TPU v7x, 128 devices: a whole 4x4x4 slice. The times are simulated.
128 devices in a mesh: fsdp: 8 (over z, core), emb: 16 (over y, x).
Axes of the slice: x: 4, y: 4, z: 4, core: 2. Of those that a mesh axis runs over, the one named last changes fastest.
Arguments:
- item_table: float32 [524288, 256], P(('fsdp', 'emb')), may hold values from -6 to 6
- item_owner: int32 [128, 1024, 1], P(('fsdp', 'emb')), may hold values from 0 to 127; in each aligned block of 1024 rows (0 to 1023, 1024 to 2047, ..., all dimensions but the last counted through in order) at most 16 rows name the same one
- item_row: int32 [128, 1024], P(('fsdp', 'emb')), may hold values from 0 to 4095
- staleness: int32 [524288], P(('fsdp', 'emb')), may hold values from 0 to 3
- w_proj: bfloat16 [2, 256, 1024], P(None, 'fsdp'), may hold values from -0.375 to 0.375
- w_out: bfloat16 [2, 256, 256], P(None, 'fsdp'), may hold values from -0.375 to 0.375
- out_grad: bfloat16 [128, 1024, 256], P(('fsdp', 'emb')), may hold values from -6 to 6
Outputs:
- new_table: float32 [524288, 256], P(('fsdp', 'emb'))
- w_proj_grad: float32 [2, 256, 1024], P(None, 'fsdp')
- w_out_grad: float32 [2, 256, 256], P(None, 'fsdp')
Inputs may be any that keep to these rules, and one draw needn't show every extreme that they name: `item_owner`: in each user's history no owner is named more than 16 times, a bound that some block reaches in every draw.
All inputs are finite; a program needn't handle non-finite values.
Results may differ from a plain program's by a relative error of at most 0.023.
Values may be sent and summed in bfloat16 or wider, within the bound.
A program may use at most 128 MiB of HBM per device.

v0:
```python
import functools

import jax
import jax.numpy as jnp
from jax import lax
from jax.experimental import pallas as pl
from jax.experimental.pallas import tpu as pltpu
from jax.sharding import PartitionSpec as P

MESH = pl.DeviceIdType.MESH

DH = 64


EPSILON = 1e-05


NT = (((1,), (1,)), ((), ()))


def matmul(left, right):
    return jnp.dot(left, right, preferred_element_type=jnp.float32)


def matmul_nt(left, right):
    return lax.dot_general(left, right, NT, preferred_element_type=jnp.float32)


def to_column(row):
    same = lax.broadcasted_iota(jnp.int32, (128, 128), 0) == lax.broadcasted_iota(
        jnp.int32, (128, 128), 1
    )
    parts = [
        jnp.sum(jnp.where(same, row[:, at : at + 128], 0.0), axis=1, keepdims=True)
        for at in range(0, row.shape[1], 128)
    ]
    return parts[0] if len(parts) == 1 else jnp.concatenate(parts, axis=0)


def layers_kernel(
    target_ref,
    returned_ref,
    proj_ref,
    out_ref,
    cotangent_ref,
    outgoing_ref,
    grads_ref,
    hidden,
    hidden_inv,
    normed,
    slope,
    gate,
    queries,
    key_heads,
    value_heads,
    attn,
    score_slope,
    mix_normed,
    mix_inv,
    gated,
    gradient,
    mixture,
    grad_mix,
    grad_pre,
    grad_mix_t,
    normed_t,
    queries_t,
):
    f32, bf16 = jnp.float32, jnp.bfloat16
    block = 256
    length, width = cotangent_ref.shape
    blocks = length // block
    heads = width // DH
    slots = returned_ref.shape[0]
    layer_count = proj_ref.shape[0]
    head_of = lax.broadcasted_iota(jnp.int32, (heads, width), 1) // DH
    head_mask = (head_of == lax.broadcasted_iota(jnp.int32, (heads, width), 0)).astype(f32)
    head_mask = head_mask.astype(bf16)

    def rows(index):
        return pl.ds(pl.multiple_of(index * block, block), block)

    def head_rows(index):
        return pl.ds(pl.multiple_of(index * block * heads, block * heads), block * heads)

    def pair_of(query, key):
        return query * (query + 1) // 2 + key

    def fetch(index, carry):
        at = pl.multiple_of(index * 128, 128)
        column = to_column(target_ref[:, pl.ds(at, 128)].astype(f32))
        total = jnp.zeros((128, width), f32)
        for first in range(0, slots, 256):
            lane = lax.broadcasted_iota(jnp.int32, (128, 256), 1).astype(f32) + float(first)
            pick = (lane == column).astype(f32).astype(bf16)
            total += matmul(pick, returned_ref[first : first + 256, :])
        hidden[0, pl.ds(at, 128), :] = total.astype(bf16)
        return carry

    lax.fori_loop(0, length // 128, fetch, 0)

    def forward(layer, carry):
        def project(index, carry):
            at = rows(index)
            value = hidden[layer, at, :].astype(f32)
            center = value - jnp.mean(value, axis=1, keepdims=True)
            inverse = lax.rsqrt(jnp.mean(center * center, axis=1, keepdims=True) + EPSILON)
            norm = (center * inverse).astype(bf16)
            hidden_inv[layer, at, :] = inverse
            normed[layer, at, :] = norm
            for part in range(4):
                columns = slice(part * width, part * width + width)
                pre = matmul(norm, proj_ref[layer, :, columns])
                logistic = 0.5 + 0.5 * jnp.tanh(0.5 * pre)
                act = pre * logistic
                slope[layer, at, columns] = (logistic + act - act * logistic).astype(bf16)
                act = act.astype(bf16)
                if part == 0:
                    gate[layer, at, :] = act
                elif part == 2:
                    queries[layer, at, :] = act * jnp.asarray(0.0625, bf16)
                else:
                    store = value_heads if part == 1 else key_heads
                    for head in range(heads):
                        spot = pl.ds(
                            pl.multiple_of((index * heads + head) * block, block), block
                        )
                        store[layer, spot, :] = act * head_mask[head : head + 1, :]
            return carry

        lax.fori_loop(0, blocks, project, 0)

        def scores(query, key, masked):
            pair = pair_of(query, key)
            query_part = queries[layer, rows(query), :]
            if masked:
                visible = lax.broadcasted_iota(
                    jnp.int32, (block, block), 1
                ) <= lax.broadcasted_iota(jnp.int32, (block, block), 0)
            for head in range(heads):
                spot = pl.ds(pl.multiple_of((key * heads + head) * block, block), block)
                half = matmul_nt(query_part, key_heads[layer, spot, :])
                bend = jnp.tanh(half)
                lift = 1.0 + bend
                if masked:
                    lift = jnp.where(visible, lift, 0.0)
                columns = slice(head * block, head * block + block)
                attn[layer, pair, :, columns] = (half * lift).astype(bf16)
                score_slope[layer, pair, :, columns] = (
                    lift * (1.0 + (half - half * bend))
                ).astype(bf16)

        def attend_rows(query, carry):
            def before(key, carry):
                scores(query, key, False)
                return carry

            lax.fori_loop(0, query, before, 0)
            scores(query, query, True)
            mixture[...] = matmul(
                attn[layer, pair_of(query, query)], value_heads[layer, head_rows(query), :]
            )

            def gather_values(key, carry):
                mixture[...] += matmul(
                    attn[layer, pair_of(query, key)], value_heads[layer, head_rows(key), :]
                )
                return carry

            lax.fori_loop(0, query, gather_values, 0)
            at = rows(query)
            value = mixture[...]
            center = value - jnp.mean(value, axis=1, keepdims=True)
            inverse = lax.rsqrt(jnp.mean(center * center, axis=1, keepdims=True) + EPSILON)
            norm = center * inverse
            mix_normed[layer, at, :] = norm
            mix_inv[layer, at, :] = inverse
            gated_part = (norm * gate[layer, at, :].astype(f32)).astype(bf16)
            gated[layer, at, :] = gated_part

            @pl.when(layer < layer_count - 1)
            def _():
                branch = matmul(gated_part, out_ref[layer])
                hidden[layer + 1, at, :] = (hidden[layer, at, :].astype(f32) + branch).astype(bf16)

            return carry

        lax.fori_loop(0, blocks, attend_rows, 0)
        return carry

    lax.fori_loop(0, layer_count, forward, 0)

    gradient[...] = cotangent_ref[...].astype(f32)

    def backward(step, carry):
        layer = layer_count - 1 - step

        def through_gate(index, carry):
            at = rows(index)
            grad_round = gradient[at, :].astype(bf16)
            grad_gated = matmul_nt(grad_round, out_ref[layer])
            norm = mix_normed[layer, at, :]
            first = slope[layer, at, :width].astype(f32)
            grad_pre[at, :width] = (grad_gated * norm * first).astype(bf16)
            inner = grad_gated * gate[layer, at, :].astype(f32)
            grad = mix_inv[layer, at, :] * (
                inner
                - jnp.mean(inner, axis=1, keepdims=True)
                - norm * jnp.mean(inner * norm, axis=1, keepdims=True)
            )
            grad_mix[at, :] = grad.astype(bf16)
            grad_mix_t[:, at] = grad.T.astype(bf16)
            normed_t[:, at] = normed[layer, at, :].T
            queries_t[:, at] = queries[layer, at, :].T
            return carry

        lax.fori_loop(0, blocks, through_gate, 0)

        gw_out = lax.dot_general(
            gated[layer],
            gradient[...].astype(bf16),
            (((0,), (0,)), ((), ())),
            preferred_element_type=jnp.float32,
        ).astype(bf16)
        depth = grads_ref.shape[3]
        for part in range(8):
            grads_ref[part % 2, part // 2, layer, :, 4 * width :] = gw_out[
                part * depth : part * depth + depth
            ]

        def through_scores(query, carry):
            def one(key, carry):
                pair = pair_of(query, key)
                grad_part = grad_mix[rows(query), :]
                for head in range(heads):
                    spot = pl.ds(pl.multiple_of((key * heads + head) * block, block), block)
                    columns = slice(head * block, head * block + block)
                    grad = matmul_nt(grad_part, value_heads[layer, spot, :])
                    score_slope[layer, pair, :, columns] = (
                        grad * score_slope[layer, pair, :, columns].astype(f32)
                    ).astype(bf16)
                return carry

            lax.fori_loop(0, query + 1, one, 0)
            mixture[...] = jnp.zeros_like(mixture)

            def gather_keys(key, carry):
                mixture[...] += matmul(
                    score_slope[layer, pair_of(query, key)], key_heads[layer, head_rows(key), :]
                )
                return carry

            lax.fori_loop(0, query + 1, gather_keys, 0)
            at = rows(query)
            third = slope[layer, at, 2 * width : 3 * width].astype(f32)
            grad_pre[at, 2 * width : 3 * width] = (mixture[...] * 0.0625 * third).astype(bf16)
            return carry

        lax.fori_loop(0, blocks, through_scores, 0)

        def through_keys(key, carry):
            at = rows(key)
            for which in range(2):
                left = (grad_mix_t, queries_t)[which]
                right = (attn, score_slope)[which]
                for head in range(heads):
                    columns = slice(head * block, head * block + block)
                    lines = slice(head * DH, head * DH + DH)

                    def add(query, total):
                        return total + matmul(
                            left[lines, rows(query)],
                            right[layer, pair_of(query, key), :, columns],
                        )

                    total = lax.fori_loop(key, blocks, add, jnp.zeros((DH, block), f32))
                    mixture[lines, :] = total
                part = (1, 3)[which]
                span = slice(part * width, part * width + width)
                grad_pre[at, span] = (mixture[...].T * slope[layer, at, span].astype(f32)).astype(
                    bf16
                )
            return carry

        lax.fori_loop(0, blocks, through_keys, 0)

        for part in range(4):
            span = slice(part * width, part * width + width)
            gw_proj = matmul(normed_t[...], grad_pre[:, span]).astype(bf16)
            for piece in range(8):
                grads_ref[piece % 2, piece // 2, layer, :, span] = gw_proj[
                    piece * depth : piece * depth + depth
                ]

        def through_norm(index, carry):
            at = rows(index)
            grad_normed = matmul_nt(grad_pre[at, :], proj_ref[layer])
            norm = normed[layer, at, :].astype(f32)
            gradient[at, :] = gradient[at, :] + hidden_inv[layer, at, :] * (
                grad_normed
                - jnp.mean(grad_normed, axis=1, keepdims=True)
                - norm * jnp.mean(grad_normed * norm, axis=1, keepdims=True)
            )
            return carry

        lax.fori_loop(0, blocks, through_norm, 0)
        return carry

    lax.fori_loop(0, layer_count, backward, 0)

    def give_back(index, carry):
        at = pl.ds(pl.multiple_of(index * 128, 128), 128)
        total = jnp.zeros((128, width), f32)
        for first in range(0, length, 256):
            spot = lax.broadcasted_iota(jnp.int32, (128, 256), 0) + index * 128
            pick = (spot == target_ref[:, first : first + 256]).astype(f32).astype(bf16)
            total += matmul(pick, gradient[first : first + 256, :].astype(bf16))
        outgoing_ref[at, :] = total.astype(bf16)
        return carry

    lax.fori_loop(0, slots // 128, give_back, 0)


def run_layers(target, returned, proj_all, out_all, cotangent, depth):
    layer_count, width, columns = proj_all.shape
    length = cotangent.shape[0]
    blocks = length // 256
    pairs = blocks * (blocks + 1) // 2
    heads = width // DH
    f32, bf16 = jnp.float32, jnp.bfloat16
    vmem = pl.BlockSpec(memory_space=pltpu.VMEM)
    return pl.pallas_call(
        layers_kernel,
        out_shape=(
            jax.ShapeDtypeStruct(returned.shape, bf16),
            jax.ShapeDtypeStruct((2, 4, layer_count, depth, columns + width), bf16),
        ),
        in_specs=[vmem] * 5,
        out_specs=(vmem, vmem),
        scratch_shapes=[
            pltpu.VMEM((layer_count, length, width), bf16),
            pltpu.VMEM((layer_count, length, 1), f32),
            pltpu.VMEM((layer_count, length, width), bf16),
            pltpu.VMEM((layer_count, length, columns), bf16),
            pltpu.VMEM((layer_count, length, width), bf16),
            pltpu.VMEM((layer_count, length, width), bf16),
            pltpu.VMEM((layer_count, length * heads, width), bf16),
            pltpu.VMEM((layer_count, length * heads, width), bf16),
            pltpu.VMEM((layer_count, pairs, 256, 256 * heads), bf16),
            pltpu.VMEM((layer_count, pairs, 256, 256 * heads), bf16),
            pltpu.VMEM((layer_count, length, width), f32),
            pltpu.VMEM((layer_count, length, 1), f32),
            pltpu.VMEM((layer_count, length, width), bf16),
            pltpu.VMEM((length, width), f32),
            pltpu.VMEM((256, width), f32),
            pltpu.VMEM((length, width), bf16),
            pltpu.VMEM((length, columns), bf16),
            pltpu.VMEM((width, length), bf16),
            pltpu.VMEM((width, length), bf16),
            pltpu.VMEM((width, length), bf16),
        ],
        compiler_params=pltpu.CompilerParams(vmem_limit_bytes=60 << 20),
        name="layers",
    )(target, returned, proj_all, out_all, cotangent)


def ask_owners(payload):
    return lax.all_to_all(payload, ("fsdp", "emb"), split_axis=0, concat_axis=0, tiled=True)


def return_rows(payload):
    return lax.all_to_all(payload, ("fsdp", "emb"), split_axis=0, concat_axis=0, tiled=True)


def device_of(index, emb_count):
    return (index // emb_count, lax.rem(index, emb_count))


def greet(me, owners, emb_count):
    barrier = pltpu.get_barrier_semaphore()

    def hello(step, carry):
        other = lax.rem(me + step, owners)
        pl.semaphore_signal(
            barrier, inc=1, device_id=device_of(other, emb_count), device_id_type=MESH
        )
        return carry

    lax.fori_loop(1, owners, hello, 0)
    return barrier


def collect_kernel(
    owners,
    emb_count,
    capacity,
    outgoing_ref,
    grads_ref,
    incoming_ref,
    total_ref,
    pair_in,
    pair_sum,
    z_in,
    z_sum,
    x_in,
    y_all,
    x_all,
    row_send,
    row_recv,
    own_sem,
    pair_sems,
    z_send,
    z_recv,
    x_send,
    x_recv,
    y_send,
    y_recv,
    g_send,
    g_recv,
):
    fsdp_at = lax.axis_index("fsdp")
    emb_at = lax.axis_index("emb")
    me = fsdp_at * emb_count + emb_at
    z_at = fsdp_at // 2
    core = lax.rem(fsdp_at, 2)
    y_at = emb_at // 4
    x_at = lax.rem(emb_at, 4)
    barrier = greet(me, owners, emb_count)
    pl.semaphore_wait(barrier, owners - 1)

    pair = pltpu.make_async_remote_copy(
        src_ref=grads_ref.at[1 - core],
        dst_ref=pair_in,
        send_sem=pair_sems.at[0],
        recv_sem=pair_sems.at[1],
        device_id=(z_at * 2 + 1 - core, emb_at),
        device_id_type=MESH,
    )
    pair.start()

    def send_rows(step, carry):
        other = lax.rem(me + step, owners)
        pltpu.make_async_remote_copy(
            src_ref=outgoing_ref.at[pl.ds(other * capacity, capacity)],
            dst_ref=incoming_ref.at[pl.ds(me * capacity, capacity)],
            send_sem=row_send,
            recv_sem=row_recv,
            device_id=device_of(other, emb_count),
            device_id_type=MESH,
        ).start()
        return carry

    lax.fori_loop(1, owners, send_rows, 0)
    own_rows = pl.ds(me * capacity, capacity)
    own = pltpu.make_async_copy(outgoing_ref.at[own_rows], incoming_ref.at[own_rows], own_sem)
    own.start()

    pair.wait()
    for z in range(4):
        for layer in range(2):
            pair_sum[z, layer] = (
                grads_ref[core, z, layer].astype(jnp.float32)
                + pair_in[z, layer].astype(jnp.float32)
            ).astype(jnp.bfloat16)
    z_copies = []
    for k in range(3):
        to = lax.rem(z_at + k + 1, 4)
        copy = pltpu.make_async_remote_copy(
            src_ref=pair_sum.at[to],
            dst_ref=z_in.at[k],
            send_sem=z_send.at[k],
            recv_sem=z_recv.at[k],
            device_id=(to * 2 + core, emb_at),
            device_id_type=MESH,
        )
        copy.start()
        z_copies.append(copy)
    for copy in z_copies:
        copy.wait()
    for part in range(4):
        rows = slice(part % 2 * 16, part % 2 * 16 + 16)
        value = pair_sum[z_at, part // 2, rows].astype(jnp.float32)
        for k in range(3):
            value += z_in[k, part // 2, rows].astype(jnp.float32)
        z_sum[part] = value.astype(jnp.bfloat16)

    x_copies = []
    for k in range(3):
        to = lax.rem(x_at + k + 1, 4)
        copy = pltpu.make_async_remote_copy(
            src_ref=z_sum.at[to],
            dst_ref=x_in.at[k],
            send_sem=x_send.at[k],
            recv_sem=x_recv.at[k],
            device_id=(fsdp_at, y_at * 4 + to),
            device_id_type=MESH,
        )
        copy.start()
        x_copies.append(copy)
    for copy in x_copies:
        copy.wait()
    value = z_sum[x_at].astype(jnp.float32)
    for k in range(3):
        value += x_in[k].astype(jnp.float32)
    y_all[y_at] = value.astype(jnp.bfloat16)

    y_copies = []
    for k in range(3):
        to = lax.rem(y_at + k + 1, 4)
        copy = pltpu.make_async_remote_copy(
            src_ref=y_all.at[y_at],
            dst_ref=y_all.at[y_at],
            send_sem=y_send.at[k],
            recv_sem=y_recv.at[k],
            device_id=(fsdp_at, to * 4 + x_at),
            device_id_type=MESH,
        )
        copy.start()
        y_copies.append(copy)
    for copy in y_copies:
        copy.wait()
    value = y_all[0].astype(jnp.float32)
    for y in range(1, 4):
        value += y_all[y].astype(jnp.float32)
    x_all[x_at] = value.astype(jnp.bfloat16)

    g_copies = []
    for k in range(3):
        to = lax.rem(x_at + k + 1, 4)
        copy = pltpu.make_async_remote_copy(
            src_ref=x_all.at[x_at],
            dst_ref=x_all.at[x_at],
            send_sem=g_send.at[k],
            recv_sem=g_recv.at[k],
            device_id=(fsdp_at, y_at * 4 + to),
            device_id_type=MESH,
        )
        copy.start()
        g_copies.append(copy)
    for copy in g_copies:
        copy.wait()
    for part in range(4):
        total_ref[part] = x_all[part]

    others = pl.ds(0, (owners - 1) * capacity)
    pltpu.make_async_copy(outgoing_ref.at[others], outgoing_ref.at[others], row_send).wait()
    pltpu.make_async_copy(incoming_ref.at[others], incoming_ref.at[others], row_recv).wait()
    own.wait()


def collect(outgoing, grads, owners, emb_count, capacity):
    columns = grads.shape[-1]
    depth = grads.shape[-2]
    bf16 = jnp.bfloat16
    vmem = pl.BlockSpec(memory_space=pltpu.VMEM)
    three = pltpu.SemaphoreType.DMA((3,))
    return pl.pallas_call(
        functools.partial(collect_kernel, owners, emb_count, capacity),
        out_shape=(
            jax.ShapeDtypeStruct(outgoing.shape, bf16),
            jax.ShapeDtypeStruct((4, 16, columns), bf16),
        ),
        in_specs=[vmem, vmem],
        out_specs=(vmem, vmem),
        scratch_shapes=[
            pltpu.VMEM((4, 2, depth, columns), bf16),
            pltpu.VMEM((4, 2, depth, columns), bf16),
            pltpu.VMEM((3, 2, depth, columns), bf16),
            pltpu.VMEM((4, 16, columns), bf16),
            pltpu.VMEM((3, 16, columns), bf16),
            pltpu.VMEM((4, 16, columns), bf16),
            pltpu.VMEM((4, 16, columns), bf16),
            pltpu.SemaphoreType.DMA,
            pltpu.SemaphoreType.DMA,
            pltpu.SemaphoreType.DMA,
            pltpu.SemaphoreType.DMA((2,)),
            three,
            three,
            three,
            three,
            three,
            three,
            three,
            three,
        ],
        compiler_params=pltpu.CompilerParams(
            collective_id=1, has_side_effects=True, vmem_limit_bytes=32 << 20
        ),
        name="collect",
    )(outgoing, grads)


def update_kernel(block, table_ref, requested_ref, stale_ref, incoming_ref, new_ref):
    count = requested_ref.shape[1]
    first = pl.program_id(0) * block
    row = first + lax.broadcasted_iota(jnp.int32, (block, count), 0)
    pick = (row == requested_ref[...]).astype(jnp.float32).astype(jnp.bfloat16)
    grad = jnp.dot(pick, incoming_ref[...], preferred_element_type=jnp.float32)
    rate = 0.5 / (1.0 + stale_ref[...].astype(jnp.float32))
    same = lax.broadcasted_iota(jnp.int32, (128, 128), 0) == lax.broadcasted_iota(
        jnp.int32, (128, 128), 1
    )
    for part in range(block // 128):
        rows = slice(part * 128, part * 128 + 128)
        spread = jnp.where(same, rate[0, part : part + 1, :], 0.0)
        column = jnp.sum(spread, axis=1, keepdims=True)
        new_ref[rows, :] = table_ref[rows, :] - column * grad[rows, :]


def update_table(table, requested, staleness, incoming):
    rows, width = table.shape
    block = 512
    count = incoming.shape[0]
    parts = block // 128
    return pl.pallas_call(
        functools.partial(update_kernel, block),
        out_shape=jax.ShapeDtypeStruct(table.shape, jnp.float32),
        grid=(rows // block,),
        in_specs=[
            pl.BlockSpec((block, width), lambda i: (i, 0)),
            pl.BlockSpec((1, count), lambda i: (0, 0)),
            pl.BlockSpec((1, parts, 128), lambda i: (i, 0, 0)),
            pl.BlockSpec((count, width), lambda i: (0, 0)),
        ],
        out_specs=pl.BlockSpec((block, width), lambda i: (i, 0)),
        compiler_params=pltpu.CompilerParams(vmem_limit_bytes=48 << 20),
        name="update_table",
    )(
        table,
        requested.reshape(1, count),
        staleness.reshape(rows // block, parts, 128),
        incoming,
    )


def local(item_table, item_owner, item_row, staleness, w_proj, w_out, out_grad):
    fsdp_count = lax.axis_size("fsdp")
    emb_count = lax.axis_size("emb")
    owners = fsdp_count * emb_count
    length = item_row.shape[1]
    capacity = 2 * length // owners
    width = item_table.shape[1]
    owner_of = item_owner[0, :, 0]
    offset = item_row[0]
    member = (owner_of[:, None] == jnp.arange(owners, dtype=jnp.int32)[None, :]).astype(jnp.int32)
    earlier = jnp.cumsum(member, axis=0) - member
    slot_index = jnp.sum(earlier * member, axis=1)
    target = owner_of * capacity + slot_index
    request = (
        jnp.full((owners * capacity,), -1, jnp.int32)
        .at[target]
        .set(offset)
        .reshape(owners, capacity)
    )
    requested = ask_owners(request)
    present = requested >= 0
    safe_rows = jnp.where(present, requested, 0)
    looked_up = jnp.where(present[:, :, None], item_table[safe_rows], 0.0).astype(jnp.bfloat16)
    returned = return_rows(looked_up)
    proj_all, out_all = (
        lax.all_gather(w_proj, "fsdp", axis=1, tiled=True),
        lax.all_gather(w_out, "fsdp", axis=1, tiled=True),
    )
    layer_count, depth = w_proj.shape[:2]
    outgoing, grads = run_layers(
        target.reshape(1, length),
        returned.reshape(owners * capacity, width),
        proj_all,
        out_all,
        out_grad[0],
        depth,
    )
    columns = grads.shape[-1]
    incoming, total = collect(outgoing, grads, owners, emb_count, capacity)
    new_table = update_table(item_table, requested, staleness, incoming)
    norm_scale = (owners * length) ** (-0.5)
    total = total.reshape(layer_count, depth, columns).astype(jnp.float32) * norm_scale
    split = w_proj.shape[-1]
    return (new_table, total[:, :, :split], total[:, :, split:])


def solution(mesh):
    return jax.shard_map(
        local,
        mesh=mesh,
        in_specs=(
            P(("fsdp", "emb"), None),
            P(("fsdp", "emb"), None, None),
            P(("fsdp", "emb"), None),
            P(("fsdp", "emb")),
            P(None, "fsdp", None),
            P(None, "fsdp", None),
            P(("fsdp", "emb"), None, None),
        ),
        out_specs=(P(("fsdp", "emb"), None), P(None, "fsdp", None), P(None, "fsdp", None)),
        check_vma=False,
    )
```

profile of v0, /device:TPU:0, one launch (start us, length us, event | category | flops | bytes accessed | tf_op | source)
XLA Modules:
  0.0 223.3 jit_solution(5121929690917144807)
XLA Ops:
  7.2 0.8 copy.16
  8.0 0.2 fusion.2
  8.2 0.1 copy.17
  8.4 1.0 fusion.1
  9.4 0.7 compare_select_fusion.2
  10.1 4.5 %scatter_custom_fusion = s32[2048]{0:T(1024)S(1)} fusion(s32[1024]{0:T(1024)S(1)} %bitcast.44, s32[1024]{0:T(1024)} %bitcast.45, s32[]{:T(128)} %constant.7.clone.1), kind=kCustom, calls=%fused_computation.21 | custom fusion | bytes 8704 | tf_op jit(solution)/shard_map/scatter | solution.py:652
  14.6 0.7 all_to_all.11
  15.3 11.1 %all-to-all-start = ((s32[128,1,16]{2,1,0:T(1,128)}), s32[128,1,16]{2,1,0:T(1,128)S(1)}, u32[]{:S(2)}, u32[]{:S(2)}) async-start(s32[128,1,16]{2,1,0:T(1,128)} %bitcast.9), calls=%async_computation | async-start | bytes 131072 | tf_op jit(solution)/shard_map/all_to_all | solution.py:368
  26.5 0.0 all-gather.2.cloned.1.call-start
  26.5 0.7 all-gather.2.cloned.1.call-update
  27.2 8.7 %all-to-all-done = s32[128,1,16]{2,1,0:T(1,128)S(1)} async-done(((s32[128,1,16]{2,1,0:T(1,128)}), s32[128,1,16]{2,1,0:T(1,128)S(1)}, u32[]{:S(2)}, u32[]{:S(2)}) %all-to-all-start) | async-done | bytes 8224 | tf_op jit(solution)/shard_map/all_to_all | solution.py:368
  35.9 0.1 reshape.128
  36.0 0.1 copy.20
  36.2 8.8 %gather_fusion = bf16[2048,256]{1,0:T(8,128)(2,1)S(1)} fusion(f32[4096,256]{1,0:T(8,128)} %table_ref.1, s32[2048]{0:T(1024)S(1)} %broadcast_clamp_fusion), kind=kCustom, calls=%fused_computation | custom fusion | bytes 2105344 | tf_op jit(solution)/shard_map/gather | solution.py:658
  45.0 0.0 copy-start.6
  45.0 0.0 copy-start.5
  45.0 1.2 select_convert_fusion
  46.3 0.0 copy-start.3
  46.3 4.8 %all-to-all-start.1 = ((bf16[128,16,256]{2,1,0:T(8,128)(2,1)}), bf16[128,16,256]{2,1,0:T(8,128)(2,1)S(1)}, u32[]{:S(2)}, u32[]{:S(2)}) async-start(bf16[128,16,256]{2,1,0:T(8,128)(2,1)} %select_convert_fusion), calls=%async_computation.1 | async-start | bytes 2097152 | tf_op jit(solution)/shard_map/all_to_all | solution.py:372
  51.0 0.0 copy-done.6
  51.1 17.8 %all_gather.7.out_ref = bf16[2,256,256]{2,1,0:T(8,128)(2,1)} all-gather(bf16[2,32,256]{2,1,0:T(8,128)(2,1)S(1)} %copy-done.6), channel_id=1, replica_groups=mesh['fsdp'=8,'emb'=16] {'fsdp'}, dimensions={1}, use_global_device_ids=true | all-gather | bytes 294912 | tf_op jit(solution)/shard_map/all_gather | solution.py:662
  68.9 0.0 copy-done.5
  68.9 0.6 bitcast_add_fusion.target_ref
  69.5 0.5 broadcast.101
  70.0 0.8 reduce.3
  70.8 0.1 reshape.123.requested_ref
  70.9 0.0 all-to-all-done.1
  70.9 0.0 copy-start.4
  70.9 0.0 all-gather.2.cloned.1.call-done.proj_ref
  71.0 1.0 copy-done.4
  72.0 84.4 %layers.1 = (bf16[2048,256]{1,0:T(8,128)(2,1)}, bf16[2,4,2,32,1280]{4,3,2,1,0:T(8,128)(2,1)}) custom-call(s32[1,1024]{1,0:T(1,128)} %bitcast_add_fusion.target_ref, bf16[2048,256]{1,0:T(8,128)(2,1)} %bitcast.35, bf16[2,256,1024]{2,1,0:T(8,128)(2,1)} %all-gather.2.cloned.1.call-done.proj_ref, bf16[2,256,256]{2,1,0:T(8,128)(2,1)} %all_gather.7.out_ref, ...), custom_call_target="tpu_custom_call" | custom-call | tf_op jit(solution)/shard_map/layers/pallas_call | solution.py:332
  156.3 0.0 copy-start.1
  156.3 1.3 copy-done.1
  157.6 0.0 copy-start.2
  157.6 1.2 copy-done.2
  158.9 47.3 %collect.1 = (bf16[2048,256]{1,0:T(8,128)(2,1)S(1)}, bf16[4,16,1280]{2,1,0:T(8,128)(2,1)S(1)}) custom-call(bf16[2048,256]{1,0:T(8,128)(2,1)S(1)} %copy-done.2, bf16[2,4,2,32,1280]{4,3,2,1,0:T(8,128)(2,1)S(1)} %copy-done.1), custom_call_target="tpu_custom_call" | custom-call | tf_op jit(solution)/shard_map/collect/pallas_call | solution.py:557
  206.2 0.7 slice.20
  206.9 0.6 slice.21
  207.6 0.0 copy-done.3
  207.6 0.0 copy-start
  207.6 2.2 copy-done
  209.8 6.7 %update_table.1 = f32[4096,256]{1,0:T(8,128)} custom-call(f32[4096,256]{1,0:T(8,128)S(1)} %copy-done, s32[1,2048]{1,0:T(1,128)S(1)} %reshape.123.requested_ref, s32[8,4,128]{2,1,0:T(4,128)S(1)} %bitcast.33, bf16[2048,256]{1,0:T(8,128)(2,1)S(1)} %get-tuple-element.9.incoming_ref), custom_call_target="tpu_custom_call" | custom-call | tf_op jit(solution)/shard_map/update_table/pallas_call | solution.py:615
  (9 shorter events, 0.2 us)
Async XLA Ops:
  15.3 20.6 %all-to-all-start = ((s32[128,1,16]{2,1,0:T(1,128)}), s32[128,1,16]{2,1,0:T(1,128)S(1)}, u32[]{:S(2)}, u32[]{:S(2)}) async-start(s32[128,1,16]{2,1,0:T(1,128)} %bitcast.9), calls=%async_computation | async-start | bytes 131072 | tf_op jit(solution)/shard_map/all_to_all | solution.py:368
  26.5 44.5 %all-gather.2.cloned.1.call-start = ((), (), s32[]{:S(2)}) async-start(), calls=%async_computation.2 | async-start | bytes 1179648 | tf_op jit(solution)/shard_map/all_gather | solution.py:661
  45.0 6.0 %copy-start.6 = (bf16[2,32,256]{2,1,0:T(8,128)(2,1)S(1)}, bf16[2,32,256]{2,1,0:T(8,128)(2,1)}, u32[]{:S(2)}) copy-start(bf16[2,32,256]{2,1,0:T(8,128)(2,1)} %param.12) | copy-start | bytes 98308
  45.0 23.9 %copy-start.5 = (s32[1,1024,1]{1,2,0:T(1,128)S(1)}, s32[1,1024,1]{1,2,0:T(1,128)}, u32[]{:S(2)}) copy-start(s32[1,1024,1]{1,2,0:T(1,128)} %param.8) | copy-start | bytes 12292
  46.3 161.3 %copy-start.3 = (s32[4096]{0:T(1024)S(1)}, s32[4096]{0:T(1024)}, u32[]{:S(2)}) copy-start(s32[4096]{0:T(1024)} %param.10) | copy-start | bytes 49156
  46.3 24.6 %all-to-all-start.1 = ((bf16[128,16,256]{2,1,0:T(8,128)(2,1)}), bf16[128,16,256]{2,1,0:T(8,128)(2,1)S(1)}, u32[]{:S(2)}, u32[]{:S(2)}) async-start(bf16[128,16,256]{2,1,0:T(8,128)(2,1)} %select_convert_fusion), calls=%async_computation.1 | async-start | bytes 2097152 | tf_op jit(solution)/shard_map/all_to_all | solution.py:372
  70.9 1.0 copy-start.4
  156.3 1.3 copy-start.1
  157.6 1.2 copy-start.2
  207.6 2.2 copy-start
Sparse Core Ops, SparseCore 0:
  29.0 24.6 all-gather.1
where the time goes:
time: 224 us; the launch traced here: 223 us
  Pallas kernels  138 us (62%)
  local copies, waits for them, and re-layouts  22.9 us (10%)
  blocking collectives  17.8 us (8%)
  starting transfers between devices  15.9 us (7%)
  between operations  14.2 us (6%)
  waiting for transfers between devices  9.37 us (4%)
  other arithmetic  4.71 us (2%)
    pallas_call x1, Pallas kernels, run_layers(): pl.pallas_call(layers_kernel, out_shape=(jax.ShapeDtypeStruct(returned.sh...  84.4 us
    pallas_call x1, Pallas kernels, collect(): pl.pallas_call(functools.partial(collect_kernel, owners, emb_count, capac...  47.3 us
    all_gather x1, blocking collectives, local(): lax.all_gather(w_out, 'fsdp', axis=1, tiled=True)  17.8 us
    all_to_all x1, starting transfers between devices, ask_owners(): lax.all_to_all(payload, ('fsdp', 'emb'), split_axis=0, concat_axis=0, til...  11.1 us
    gather x1, local copies, waits for them, and re-layouts, local(): item_table[safe_rows]  8.83 us
    all_to_all x1, waiting for transfers between devices, ask_owners(): lax.all_to_all(payload, ('fsdp', 'emb'), split_axis=0, concat_axis=0, til...  8.67 us
    pallas_call x1, Pallas kernels, update_table(): pl.pallas_call(functools.partial(update_kernel, block), out_shape=jax.Sha...  6.74 us
    unnamed x14, local copies, waits for them, and re-layouts  5.73 us
  transfers between devices with their start and end apart: 3, of which 1 were waited for; matrix products, arithmetic and copies ran while one was open for 6% of the time, Pallas kernels for 0%

commit v1 on v0

--- a/solution.py
+++ b/solution.py
@@ -40,8 +40,7 @@
 def layers_kernel(
     target_ref,
     returned_ref,
-    proj_ref,
-    out_ref,
+    weights_ref,
     cotangent_ref,
     outgoing_ref,
     grads_ref,
@@ -65,6 +64,8 @@
     grad_mix_t,
     normed_t,
     queries_t,
+    keys_t,
+    values_t,
 ):
     f32, bf16 = jnp.float32, jnp.bfloat16
     block = 256
@@ -72,7 +73,7 @@
     blocks = length // block
     heads = width // DH
     slots = returned_ref.shape[0]
-    layer_count = proj_ref.shape[0]
+    layer_count = weights_ref.shape[0]
     head_of = lax.broadcasted_iota(jnp.int32, (heads, width), 1) // DH
     head_mask = (head_of == lax.broadcasted_iota(jnp.int32, (heads, width), 0)).astype(f32)
     head_mask = head_mask.astype(bf16)
@@ -110,7 +111,7 @@
             normed[layer, at, :] = norm
             for part in range(4):
                 columns = slice(part * width, part * width + width)
-                pre = matmul(norm, proj_ref[layer, :, columns])
+                pre = matmul(norm, weights_ref[layer, :, columns])
                 logistic = 0.5 + 0.5 * jnp.tanh(0.5 * pre)
                 act = pre * logistic
                 slope[layer, at, columns] = (logistic + act - act * logistic).astype(bf16)
@@ -137,6 +138,7 @@
                 visible = lax.broadcasted_iota(
                     jnp.int32, (block, block), 1
                 ) <= lax.broadcasted_iota(jnp.int32, (block, block), 0)
+            parts = []
             for head in range(heads):
                 spot = pl.ds(pl.multiple_of((key * heads + head) * block, block), block)
                 half = matmul_nt(query_part, key_heads[layer, spot, :])
@@ -145,29 +147,24 @@
                 if masked:
                     lift = jnp.where(visible, lift, 0.0)
                 columns = slice(head * block, head * block + block)
-                attn[layer, pair, :, columns] = (half * lift).astype(bf16)
+                part = (half * lift).astype(bf16)
+                parts.append(part)
+                attn[layer, pair, :, columns] = part
                 score_slope[layer, pair, :, columns] = (
                     lift * (1.0 + (half - half * bend))
                 ).astype(bf16)
+            return matmul(
+                jnp.concatenate(parts, axis=1), value_heads[layer, head_rows(key), :]
+            )
 
         def attend_rows(query, carry):
+            mixture[...] = scores(query, query, True)
+
             def before(key, carry):
-                scores(query, key, False)
+                mixture[...] += scores(query, key, False)
                 return carry
 
             lax.fori_loop(0, query, before, 0)
-            scores(query, query, True)
-            mixture[...] = matmul(
-                attn[layer, pair_of(query, query)], value_heads[layer, head_rows(query), :]
-            )
-
-            def gather_values(key, carry):
-                mixture[...] += matmul(
-                    attn[layer, pair_of(query, key)], value_heads[layer, head_rows(key), :]
-                )
-                return carry
-
-            lax.fori_loop(0, query, gather_values, 0)
             at = rows(query)
             value = mixture[...]
             center = value - jnp.mean(value, axis=1, keepdims=True)
@@ -180,7 +177,7 @@
 
             @pl.when(layer < layer_count - 1)
             def _():
-                branch = matmul(gated_part, out_ref[layer])
+                branch = matmul(gated_part, weights_ref[layer, :, 4 * width :])
                 hidden[layer + 1, at, :] = (hidden[layer, at, :].astype(f32) + branch).astype(bf16)
 
             return carry
@@ -198,7 +195,7 @@
         def through_gate(index, carry):
             at = rows(index)
             grad_round = gradient[at, :].astype(bf16)
-            grad_gated = matmul_nt(grad_round, out_ref[layer])
+            grad_gated = matmul_nt(grad_round, weights_ref[layer, :, 4 * width :])
             norm = mix_normed[layer, at, :]
             first = slope[layer, at, :width].astype(f32)
             grad_pre[at, :width] = (grad_gated * norm * first).astype(bf16)
@@ -228,29 +225,35 @@
                 part * depth : part * depth + depth
             ]
 
+        keys_t[...] = jnp.zeros_like(keys_t)
+        values_t[...] = jnp.zeros_like(values_t)
+
         def through_scores(query, carry):
+            mixture[...] = jnp.zeros_like(mixture)
+
             def one(key, carry):
                 pair = pair_of(query, key)
-                grad_part = grad_mix[rows(query), :]
+                here = rows(query)
+                there = rows(key)
+                grad_part = grad_mix[here, :]
+                parts = []
                 for head in range(heads):
                     spot = pl.ds(pl.multiple_of((key * heads + head) * block, block), block)
                     columns = slice(head * block, head * block + block)
+                    lines = slice(head * DH, head * DH + DH)
                     grad = matmul_nt(grad_part, value_heads[layer, spot, :])
-                    score_slope[layer, pair, :, columns] = (
-                        grad * score_slope[layer, pair, :, columns].astype(f32)
-                    ).astype(bf16)
-                return carry
-
-            lax.fori_loop(0, query + 1, one, 0)
-            mixture[...] = jnp.zeros_like(mixture)
-
-            def gather_keys(key, carry):
+                    values_t[lines, there] += matmul(
+                        grad_mix_t[lines, here], attn[layer, pair, :, columns]
+                    )
+                    part = (grad * score_slope[layer, pair, :, columns].astype(f32)).astype(bf16)
+                    parts.append(part)
+                    keys_t[lines, there] += matmul(queries_t[lines, here], part)
                 mixture[...] += matmul(
-                    score_slope[layer, pair_of(query, key)], key_heads[layer, head_rows(key), :]
+                    jnp.concatenate(parts, axis=1), key_heads[layer, head_rows(key), :]
                 )
                 return carry
 
-            lax.fori_loop(0, query + 1, gather_keys, 0)
+            lax.fori_loop(0, query + 1, one, 0)
             at = rows(query)
             third = slope[layer, at, 2 * width : 3 * width].astype(f32)
             grad_pre[at, 2 * width : 3 * width] = (mixture[...] * 0.0625 * third).astype(bf16)
@@ -260,24 +263,9 @@
 
         def through_keys(key, carry):
             at = rows(key)
-            for which in range(2):
-                left = (grad_mix_t, queries_t)[which]
-                right = (attn, score_slope)[which]
-                for head in range(heads):
-                    columns = slice(head * block, head * block + block)
-                    lines = slice(head * DH, head * DH + DH)
-
-                    def add(query, total):
-                        return total + matmul(
-                            left[lines, rows(query)],
-                            right[layer, pair_of(query, key), :, columns],
-                        )
-
-                    total = lax.fori_loop(key, blocks, add, jnp.zeros((DH, block), f32))
-                    mixture[lines, :] = total
-                part = (1, 3)[which]
+            for part, total in ((1, values_t), (3, keys_t)):
                 span = slice(part * width, part * width + width)
-                grad_pre[at, span] = (mixture[...].T * slope[layer, at, span].astype(f32)).astype(
+                grad_pre[at, span] = (total[:, at].T * slope[layer, at, span].astype(f32)).astype(
                     bf16
                 )
             return carry
@@ -294,7 +282,7 @@
 
         def through_norm(index, carry):
             at = rows(index)
-            grad_normed = matmul_nt(grad_pre[at, :], proj_ref[layer])
+            grad_normed = matmul_nt(grad_pre[at, :], weights_ref[layer, :, : 4 * width])
             norm = normed[layer, at, :].astype(f32)
             gradient[at, :] = gradient[at, :] + hidden_inv[layer, at, :] * (
                 grad_normed
@@ -321,8 +309,9 @@
     lax.fori_loop(0, slots // 128, give_back, 0)
 
 
-def run_layers(target, returned, proj_all, out_all, cotangent, depth):
-    layer_count, width, columns = proj_all.shape
+def run_layers(target, returned, weights, cotangent, depth):
+    layer_count, width, columns = weights.shape
+    columns -= width
     length = cotangent.shape[0]
     blocks = length // 256
     pairs = blocks * (blocks + 1) // 2
@@ -335,7 +324,7 @@
             jax.ShapeDtypeStruct(returned.shape, bf16),
             jax.ShapeDtypeStruct((2, 4, layer_count, depth, columns + width), bf16),
         ),
-        in_specs=[vmem] * 5,
+        in_specs=[vmem] * 4,
         out_specs=(vmem, vmem),
         scratch_shapes=[
             pltpu.VMEM((layer_count, length, width), bf16),
@@ -358,18 +347,12 @@
             pltpu.VMEM((width, length), bf16),
             pltpu.VMEM((width, length), bf16),
             pltpu.VMEM((width, length), bf16),
+            pltpu.VMEM((width, length), f32),
+            pltpu.VMEM((width, length), f32),
         ],
         compiler_params=pltpu.CompilerParams(vmem_limit_bytes=60 << 20),
         name="layers",
-    )(target, returned, proj_all, out_all, cotangent)
-
-
-def ask_owners(payload):
-    return lax.all_to_all(payload, ("fsdp", "emb"), split_axis=0, concat_axis=0, tiled=True)
-
-
-def return_rows(payload):
-    return lax.all_to_all(payload, ("fsdp", "emb"), split_axis=0, concat_axis=0, tiled=True)
+    )(target, returned, weights, cotangent)
 
 
 def device_of(index, emb_count):
@@ -388,6 +371,227 @@
 
     lax.fori_loop(1, owners, hello, 0)
     return barrier
+
+
+def lookup_kernel(
+    owners,
+    emb_count,
+    capacity,
+    owner_ref,
+    offset_ref,
+    proj_ref,
+    out_ref,
+    table_ref,
+    returned_ref,
+    asked_ref,
+    target_ref,
+    weights_ref,
+    table_wide,
+    table,
+    member,
+    ask,
+    found,
+    table_sem,
+    ask_send,
+    ask_recv,
+    row_send,
+    row_recv,
+    z_send,
+    z_recv,
+    pair_send,
+    pair_recv,
+):
+    f32, bf16 = jnp.float32, jnp.bfloat16
+    fsdp_at = lax.axis_index("fsdp")
+    emb_at = lax.axis_index("emb")
+    me = fsdp_at * emb_count + emb_at
+    z_at = fsdp_at // 2
+    core = lax.rem(fsdp_at, 2)
+    barrier = greet(me, owners, emb_count)
+    load = pltpu.make_async_copy(table_ref, table_wide, table_sem)
+    load.start()
+
+    split = proj_ref.shape[2]
+    weights_ref[:, z_at, core, :, :split] = proj_ref[...]
+    weights_ref[:, z_at, core, :, split:] = out_ref[...]
+
+    length = owner_ref.shape[1]
+    owner = owner_ref[...]
+    value = offset_ref[...] + 1
+    high = (value // 64).astype(f32)
+    low = lax.rem(value, 64).astype(f32)
+    row_at = lax.broadcasted_iota(jnp.int32, (owners, 256), 0)
+    for at in range(0, length, 256):
+        member[:, at : at + 256] = (
+            (row_at == owner[:, at : at + 256]).astype(f32).astype(bf16)
+        )
+    slots = []
+    for at in range(0, length, 256):
+        earlier = jnp.zeros((owners, 256), f32)
+        for first in range(0, at + 256, 256):
+            before = (
+                lax.broadcasted_iota(jnp.int32, (256, 256), 0) + (first - at)
+                < lax.broadcasted_iota(jnp.int32, (256, 256), 1)
+            )
+            earlier += matmul(member[:, first : first + 256], before.astype(f32).astype(bf16))
+        slots.append(
+            jnp.sum(earlier * member[:, at : at + 256].astype(f32), axis=0, keepdims=True)
+        )
+    slot = jnp.concatenate(slots, axis=1)
+    target_ref[...] = owner * capacity + slot.astype(jnp.int32)
+    here = lax.broadcasted_iota(jnp.int32, (128, length), 0).astype(f32) == slot
+    request = 64.0 * matmul_nt(member[...], jnp.where(here, high, 0.0).astype(bf16))
+    request += matmul_nt(member[...], jnp.where(here, low, 0.0).astype(bf16))
+    ask[...] = request.astype(jnp.int32).reshape(ask.shape)
+
+    pl.semaphore_wait(barrier, owners - 1)
+
+    def send_ask(step, carry):
+        other = lax.rem(me + step, owners)
+        pltpu.make_async_remote_copy(
+            src_ref=ask.at[other],
+            dst_ref=asked_ref.at[me],
+            send_sem=ask_send,
+            recv_sem=ask_recv,
+            device_id=device_of(other, emb_count),
+            device_id_type=MESH,
+        ).start()
+        return carry
+
+    lax.fori_loop(1, owners, send_ask, 0)
+    z_copies = []
+    for k in range(3):
+        to = lax.rem(z_at + k + 1, 4)
+        copy = pltpu.make_async_remote_copy(
+            src_ref=weights_ref.at[:, z_at, core],
+            dst_ref=weights_ref.at[:, z_at, core],
+            send_sem=z_send.at[k],
+            recv_sem=z_recv.at[k],
+            device_id=(to * 2 + core, emb_at),
+            device_id_type=MESH,
+        )
+        copy.start()
+        z_copies.append(copy)
+    asked_ref[me] = ask[me]
+
+    load.wait()
+    rows = table.shape[0]
+
+    def narrow(index, carry):
+        at = pl.ds(pl.multiple_of(index * 512, 512), 512)
+        table[at, :] = table_wide[at, :].astype(bf16)
+        return carry
+
+    lax.fori_loop(0, rows // 512, narrow, 0)
+
+    others = pl.ds(0, owners - 1)
+    pltpu.make_async_copy(ask.at[others], ask.at[others], ask_send).wait()
+    pltpu.make_async_copy(asked_ref.at[others], asked_ref.at[others], ask_recv).wait()
+
+    group = 256 // capacity
+    groups = owners // group
+
+    def find(step, carry):
+        index = lax.rem(me // group + step, groups)
+        first_user = index * group
+        wanted = asked_ref[pl.ds(first_user, group)].astype(f32)
+        wanted = jnp.broadcast_to(wanted, (group, capacity, 128))
+        same = lax.broadcasted_iota(jnp.int32, wanted.shape, 1) == lax.broadcasted_iota(
+            jnp.int32, wanted.shape, 2
+        )
+        column = jnp.sum(jnp.where(same, wanted, 0.0), axis=2, keepdims=True)
+        column = column.reshape(256, 1) - 1.0
+        lane = lax.broadcasted_iota(jnp.int32, (256, 256), 1).astype(f32)
+        total = jnp.zeros((256, table.shape[1]), f32)
+        for first in range(0, rows, 256):
+            pick = (lane + float(first) == column).astype(f32).astype(bf16)
+            total += matmul(pick, table[first : first + 256, :])
+        found[pl.ds(pl.multiple_of(index * 256, 256), 256), :] = total.astype(bf16)
+
+        def send_rows(turn, carry):
+            user = first_user + lax.rem(me + turn, group)
+
+            @pl.when(user != me)
+            def _():
+                pltpu.make_async_remote_copy(
+                    src_ref=found.at[pl.ds(user * capacity, capacity)],
+                    dst_ref=returned_ref.at[pl.ds(me * capacity, capacity)],
+                    send_sem=row_send,
+                    recv_sem=row_recv,
+                    device_id=device_of(user, emb_count),
+                    device_id_type=MESH,
+                ).start()
+
+            return carry
+
+        lax.fori_loop(0, group, send_rows, 0)
+        return carry
+
+    lax.fori_loop(0, groups, find, 0)
+    own = pl.ds(pl.multiple_of(me * capacity, capacity), capacity)
+    returned_ref[own, :] = found[own, :]
+
+    for copy in z_copies:
+        copy.wait()
+    pair_copies = []
+    for z in range(4):
+        copy = pltpu.make_async_remote_copy(
+            src_ref=weights_ref.at[:, z, core],
+            dst_ref=weights_ref.at[:, z, core],
+            send_sem=pair_send.at[z],
+            recv_sem=pair_recv.at[z],
+            device_id=(z_at * 2 + 1 - core, emb_at),
+            device_id_type=MESH,
+        )
+        copy.start()
+        pair_copies.append(copy)
+    for copy in pair_copies:
+        copy.wait()
+    lines = pl.ds(0, (owners - 1) * capacity)
+    pltpu.make_async_copy(found.at[lines], found.at[lines], row_send).wait()
+    pltpu.make_async_copy(returned_ref.at[lines], returned_ref.at[lines], row_recv).wait()
+
+
+def look_up(owner, offset, w_proj, w_out, table, owners, emb_count, capacity):
+    bf16 = jnp.bfloat16
+    layer_count, depth, split = w_proj.shape
+    columns = split + w_out.shape[2]
+    rows, width = table.shape
+    length = owner.shape[1]
+    slots = owners * capacity
+    vmem = pl.BlockSpec(memory_space=pltpu.VMEM)
+    one = pltpu.SemaphoreType.DMA
+    return pl.pallas_call(
+        functools.partial(lookup_kernel, owners, emb_count, capacity),
+        out_shape=(
+            jax.ShapeDtypeStruct((slots, width), bf16),
+            jax.ShapeDtypeStruct((owners, 1, 128), jnp.int32),
+            jax.ShapeDtypeStruct((1, length), jnp.int32),
+            jax.ShapeDtypeStruct((layer_count, 4, 2, depth, columns), bf16),
+        ),
+        in_specs=[vmem] * 4 + [pl.BlockSpec(memory_space=pl.ANY)],
+        out_specs=(vmem,) * 4,
+        scratch_shapes=[
+            pltpu.VMEM((rows, width), jnp.float32),
+            pltpu.VMEM((rows, width), bf16),
+            pltpu.VMEM((owners, length), bf16),
+            pltpu.VMEM((owners, 1, 128), jnp.int32),
+            pltpu.VMEM((slots, width), bf16),
+            one,
+            one,
+            one,
+            one,
+            one,
+            one((3,)),
+            one((3,)),
+            one((4,)),
+            one((4,)),
+        ],
+        compiler_params=pltpu.CompilerParams(
+            collective_id=2, has_side_effects=True, vmem_limit_bytes=40 << 20
+        ),
+        name="look_up",
+    )(owner, offset, w_proj, w_out, table)
 
 
 def collect_kernel(
@@ -639,43 +843,25 @@
     owners = fsdp_count * emb_count
     length = item_row.shape[1]
     capacity = 2 * length // owners
-    width = item_table.shape[1]
-    owner_of = item_owner[0, :, 0]
-    offset = item_row[0]
-    member = (owner_of[:, None] == jnp.arange(owners, dtype=jnp.int32)[None, :]).astype(jnp.int32)
-    earlier = jnp.cumsum(member, axis=0) - member
-    slot_index = jnp.sum(earlier * member, axis=1)
-    target = owner_of * capacity + slot_index
-    request = (
-        jnp.full((owners * capacity,), -1, jnp.int32)
-        .at[target]
-        .set(offset)
-        .reshape(owners, capacity)
+    layer_count, depth, split = w_proj.shape
+    returned, asked, target, weights = look_up(
+        item_owner.reshape(1, length),
+        item_row,
+        w_proj,
+        w_out,
+        item_table,
+        owners,
+        emb_count,
+        capacity,
     )
-    requested = ask_owners(request)
-    present = requested >= 0
-    safe_rows = jnp.where(present, requested, 0)
-    looked_up = jnp.where(present[:, :, None], item_table[safe_rows], 0.0).astype(jnp.bfloat16)
-    returned = return_rows(looked_up)
-    proj_all, out_all = (
-        lax.all_gather(w_proj, "fsdp", axis=1, tiled=True),
-        lax.all_gather(w_out, "fsdp", axis=1, tiled=True),
-    )
-    layer_count, depth = w_proj.shape[:2]
-    outgoing, grads = run_layers(
-        target.reshape(1, length),
-        returned.reshape(owners * capacity, width),
-        proj_all,
-        out_all,
-        out_grad[0],
-        depth,
-    )
-    columns = grads.shape[-1]
+    columns = weights.shape[-1]
+    weights = weights.reshape(layer_count, fsdp_count * depth, columns)
+    outgoing, grads = run_layers(target, returned, weights, out_grad[0], depth)
+    requested = asked[:, 0, :capacity] - 1
     incoming, total = collect(outgoing, grads, owners, emb_count, capacity)
     new_table = update_table(item_table, requested, staleness, incoming)
     norm_scale = (owners * length) ** (-0.5)
     total = total.reshape(layer_count, depth, columns).astype(jnp.float32) * norm_scale
-    split = w_proj.shape[-1]
     return (new_table, total[:, :, :split], total[:, :, split:])
 
 

time: 224 us -> 158 us (0.71)
  blocking collectives: 17.8 us -> 0 us
  starting transfers between devices: 15.9 us -> 0 us
  between operations: 14.2 us -> 0.7 us
  waiting for transfers between devices: 9.37 us -> 0 us
  local copies, waits for them, and re-layouts: 22.9 us -> 14 us
  Pallas kernels: 138 us -> 143 us
  other arithmetic: 4.71 us -> 0.22 us
    pallas_call x0 -> x1, Pallas kernels: none -> 35.4 us  [look_up(): pl.pallas_call(functools.partial(lookup_kernel, owners, emb_count, capaci...]
    pallas_call x1, Pallas kernels: 84.4 us -> 58.7 us  [run_layers(): pl.pallas_call(layers_kernel, out_shape=(jax.ShapeDtypeStruct(returned.sh...]
    all_gather x1 -> x0, blocking collectives: 17.8 us -> none  [local(): lax.all_gather(w_out, 'fsdp', axis=1, tiled=True)]
    all_to_all x2 -> x0, starting transfers between devices: 15.9 us -> none  [the longest x1 11.1 us: ask_owners(): lax.all_to_all(payload, ('fsdp', 'emb'), split_axis=0, concat_axis=0, til...]
    gather x1 -> x0, local copies, waits for them, and re-layouts: 8.83 us -> none  [local(): item_table[safe_rows]]
    all_to_all x2 -> x0, waiting for transfers between devices: 8.67 us -> none  [the longest x1 8.67 us: ask_owners(): lax.all_to_all(payload, ('fsdp', 'emb'), split_axis=0, concat_axis=0, til...]
    unnamed x14 -> x24, local copies, waits for them, and re-layouts: 5.73 us -> 12.5 us
    pallas_call x1, Pallas kernels: 47.3 us -> 41.7 us  [collect(): pl.pallas_call(functools.partial(collect_kernel, owners, emb_count, capac...]
  transfers between devices with their start and end apart: 3 -> 0, of which waited for: 1 -> 0; matrix products, arithmetic and copies ran while one was open for 6% -> 0% of each run, Pallas kernels for 0% -> 0%
where the time goes in v1:
time: 158 us; the launch traced here: 157 us
  Pallas kernels  143 us (91%)
  local copies, waits for them, and re-layouts  14 us (9%)
    pallas_call x1, Pallas kernels, run_layers(): pl.pallas_call(layers_kernel, out_shape=(jax.ShapeDtypeStruct(returned.sh...  58.7 us
    pallas_call x1, Pallas kernels, collect(): pl.pallas_call(functools.partial(collect_kernel, owners, emb_count, capac...  41.7 us
    pallas_call x1, Pallas kernels, look_up(): pl.pallas_call(functools.partial(lookup_kernel, owners, emb_count, capaci...  35.4 us
    unnamed x24, local copies, waits for them, and re-layouts  12.5 us
    pallas_call x1, Pallas kernels, update_table(): pl.pallas_call(functools.partial(update_kernel, block), out_shape=jax.Sha...  6.74 us

profile of v1, /device:TPU:0, one launch (start us, length us, event | category | flops | bytes accessed | tf_op | source)
XLA Modules:
  0.0 157.4 jit_solution(5553138067270865819)
XLA Ops:
  0.6 0.0 copy-start
  0.6 2.2 %copy-done = f32[4096,256]{1,0:T(8,128)S(1)} copy-done((f32[4096,256]{1,0:T(8,128)S(1)}, f32[4096,256]{1,0:T(8,128)}, u32[]{:S(2)}) %copy-start) | copy-done | bytes 4194328
  2.8 0.0 copy-start.6
  2.8 0.9 copy-done.6
  3.7 0.0 copy-start.7
  3.7 0.8 copy-done.7
  4.5 0.0 copy-start.10
  4.5 0.7 copy-done.10
  5.2 0.0 copy-start.11
  5.2 0.7 copy-done.11
  5.9 0.0 copy-start.8
  5.9 35.4 %look_up.1 = (bf16[2048,256]{1,0:T(8,128)(2,1)S(1)}, s32[128,1,128]{2,1,0:T(1,128)S(1)}, s32[1,1024]{1,0:T(1,128)S(1)}, bf16[2,4,2,32,1280]{4,3,2,1,0:T(8,128)(2,1)S(1)}) custom-call(s32[1,1024]{1,0:T(1,128)S(1)} %bitcast.7, s32[1,1024]{1,0:T(1,128)S(1)} %copy-done.11, bf16[2,32,1024]{2,1,0:T(8,128)(2,1)S(1)} %copy-done.6, ...), custom_call_target="tpu_custom_call" | custom-call | tf_op jit(solution)/shard_map/look_up/pallas_call | solution.py:564
  41.3 0.0 copy-start.3
  41.3 1.0 copy-done.3
  42.4 0.0 copy-start.5
  42.4 1.0 copy-done.5
  43.3 0.0 copy-start.9
  43.3 0.6 copy-done.9
  43.9 58.7 %layers.1 = (bf16[2048,256]{1,0:T(8,128)(2,1)}, bf16[2,4,2,32,1280]{4,3,2,1,0:T(8,128)(2,1)}) custom-call(s32[1,1024]{1,0:T(1,128)} %copy-done.9, bf16[2048,256]{1,0:T(8,128)(2,1)} %copy-done.5, bf16[2,256,1280]{2,1,0:T(8,128)(2,1)} %bitcast.5, bf16[1024,256]{1,0:T(8,128)(2,1)} %bitcast.10), custom_call_target="tpu_custom_call" | custom-call | tf_op jit(solution)/shard_map/layers/pallas_call | solution.py:321
  102.6 0.0 copy-start.2
  102.6 1.3 copy-done.2
  103.9 0.0 copy-start.4
  103.9 1.2 copy-done.4
  105.1 41.7 %collect.1 = (bf16[2048,256]{1,0:T(8,128)(2,1)S(1)}, bf16[4,16,1280]{2,1,0:T(8,128)(2,1)S(1)}) custom-call(bf16[2048,256]{1,0:T(8,128)(2,1)S(1)} %copy-done.4, bf16[2,4,2,32,1280]{4,3,2,1,0:T(8,128)(2,1)S(1)} %copy-done.2), custom_call_target="tpu_custom_call" | custom-call | tf_op jit(solution)/shard_map/collect/pallas_call | solution.py:761
  146.8 0.2 add_reduce_fusion
  147.0 0.1 sub.7.requested_ref
  147.1 0.0 copy-done.8
  147.1 0.0 copy-start.1
  147.1 2.2 %copy-done.1 = f32[4096,256]{1,0:T(8,128)S(1)} copy-done((f32[4096,256]{1,0:T(8,128)S(1)}, f32[4096,256]{1,0:T(8,128)}, u32[]{:S(2)}) %copy-start.1) | copy-done | bytes 4194328
  149.3 6.7 %update_table.1 = f32[4096,256]{1,0:T(8,128)} custom-call(f32[4096,256]{1,0:T(8,128)S(1)} %copy-done.1, s32[1,2048]{1,0:T(1,128)S(1)} %sub.7.requested_ref, s32[8,4,128]{2,1,0:T(4,128)S(1)} %bitcast.6, bf16[2048,256]{1,0:T(8,128)(2,1)S(1)} %get-tuple-element.17.incoming_ref), custom_call_target="tpu_custom_call" | custom-call | tf_op jit(solution)/shard_map/update_table/pallas_call | solution.py:819
  156.1 0.7 slice.12
  156.8 0.6 slice.13
  (1 shorter events, 0.0 us)
Async XLA Ops:
  0.6 2.2 %copy-start = (f32[4096,256]{1,0:T(8,128)S(1)}, f32[4096,256]{1,0:T(8,128)}, u32[]{:S(2)}) copy-start(f32[4096,256]{1,0:T(8,128)} %table_ref.3) | copy-start | bytes 12582916
  2.8 0.9 copy-start.6
  3.7 0.8 copy-start.7
  4.5 0.7 copy-start.10
  5.2 0.7 copy-start.11
  5.9 141.2 %copy-start.8 = (s32[4096]{0:T(1024)S(1)}, s32[4096]{0:T(1024)}, u32[]{:S(2)}) copy-start(s32[4096]{0:T(1024)} %param.10) | copy-start | bytes 49156
  41.3 1.1 copy-start.3
  42.4 1.0 copy-start.5
  43.3 0.6 copy-start.9
  102.6 1.3 copy-start.2
  103.9 1.2 copy-start.4
  147.1 2.2 %copy-start.1 = (f32[4096,256]{1,0:T(8,128)S(1)}, f32[4096,256]{1,0:T(8,128)}, u32[]{:S(2)}) copy-start(f32[4096,256]{1,0:T(8,128)} %table_ref.3) | copy-start | bytes 12582916

commit v2 on v0

v2 whole, which is shorter than its diff:
```python
import functools

import jax
import jax.numpy as jnp
from jax import lax
from jax.experimental import pallas as pl
from jax.experimental.pallas import tpu as pltpu
from jax.sharding import PartitionSpec as P

MESH = pl.DeviceIdType.MESH

DH = 64


EPSILON = 1e-05


NT = (((1,), (1,)), ((), ()))


def matmul(left, right):
    return jnp.dot(left, right, preferred_element_type=jnp.float32)


def matmul_nt(left, right):
    return lax.dot_general(left, right, NT, preferred_element_type=jnp.float32)


def to_column(row):
    same = lax.broadcasted_iota(jnp.int32, (128, 128), 0) == lax.broadcasted_iota(
        jnp.int32, (128, 128), 1
    )
    parts = [
        jnp.sum(jnp.where(same, row[:, at : at + 128], 0.0), axis=1, keepdims=True)
        for at in range(0, row.shape[1], 128)
    ]
    return parts[0] if len(parts) == 1 else jnp.concatenate(parts, axis=0)


def device_of(index, emb_count):
    return (index // emb_count, lax.rem(index, emb_count))


def greet(me, owners, emb_count):
    barrier = pltpu.get_barrier_semaphore()

    def hello(step, carry):
        other = lax.rem(me + step, owners)
        pl.semaphore_signal(
            barrier, inc=1, device_id=device_of(other, emb_count), device_id_type=MESH
        )
        return carry

    lax.fori_loop(1, owners, hello, 0)
    return barrier


def step_kernel(
    owners,
    emb_count,
    capacity,
    owner_hbm,
    offset_hbm,
    proj_hbm,
    out_hbm,
    table_hbm,
    cotangent_hbm,
    incoming_ref,
    asked_ref,
    total_ref,
    owner_ref,
    offset_ref,
    proj_ref,
    out_ref,
    cotangent_ref,
    returned_ref,
    target_ref,
    weights_ref,
    member,
    ask,
    found,
    hidden,
    hidden_inv,
    normed,
    slope,
    gate,
    queries,
    key_heads,
    value_heads,
    attn,
    score_slope,
    mix_normed,
    mix_inv,
    gated,
    gradient,
    mixture,
    grad_mix,
    grad_pre,
    grad_mix_t,
    normed_t,
    queries_t,
    keys_t,
    values_t,
    grads,
    pair_in,
    z_in,
    z_sum,
    x_in,
    y_all,
    load_sems,
    ask_send,
    ask_recv,
    row_send,
    row_recv,
    grad_send,
    grad_recv,
    z_send,
    z_recv,
    pair_send,
    pair_recv,
    reduce_send,
    reduce_recv,
):
    f32, bf16 = jnp.float32, jnp.bfloat16
    fsdp_at = lax.axis_index("fsdp")
    emb_at = lax.axis_index("emb")
    me = fsdp_at * emb_count + emb_at
    z_at = fsdp_at // 2
    core = lax.rem(fsdp_at, 2)
    y_at = emb_at // 4
    x_at = lax.rem(emb_at, 4)
    barrier = greet(me, owners, emb_count)
    loads = []
    for number, (source, place) in enumerate(
        ((owner_hbm, owner_ref), (offset_hbm, offset_ref), (proj_hbm, proj_ref), (out_hbm, out_ref))
    ):
        load = pltpu.make_async_copy(source, place, load_sems.at[number])
        load.start()
        loads.append(load)
    chunk = gradient.shape[0]
    wide = (gradient, mix_normed.at[0], mix_normed.at[1], gradient)
    table_loads = [
        pltpu.make_async_copy(
            table_hbm.at[pl.ds(number * chunk, chunk)], wide[number], load_sems.at[4 + number]
        )
        for number in range(4)
    ]
    for number in range(3):
        table_loads[number].start()
    cotangent_load = pltpu.make_async_copy(cotangent_hbm, cotangent_ref, load_sems.at[8])
    cotangent_load.start()
    for load in loads:
        load.wait()

    split = proj_ref.shape[2]
    weights_ref[:, z_at, core, :, :split] = proj_ref[...]
    weights_ref[:, z_at, core, :, split:] = out_ref[...]

    length = owner_ref.shape[1]
    owner = owner_ref[...]
    value = offset_ref[...] + 1
    high = (value // 64).astype(f32)
    low = lax.rem(value, 64).astype(f32)
    row_at = lax.broadcasted_iota(jnp.int32, (owners, 256), 0)
    for at in range(0, length, 256):
        member[:, at : at + 256] = (
            (row_at == owner[:, at : at + 256]).astype(f32).astype(bf16)
        )
    slots = []
    for at in range(0, length, 256):
        earlier = jnp.zeros((owners, 256), f32)
        for first in range(0, at + 256, 256):
            before = (
                lax.broadcasted_iota(jnp.int32, (256, 256), 0) + (first - at)
                < lax.broadcasted_iota(jnp.int32, (256, 256), 1)
            )
            earlier += matmul(member[:, first : first + 256], before.astype(f32).astype(bf16))
        slots.append(
            jnp.sum(earlier * member[:, at : at + 256].astype(f32), axis=0, keepdims=True)
        )
    slot = jnp.concatenate(slots, axis=1)
    target_ref[...] = owner * capacity + slot.astype(jnp.int32)
    here = lax.broadcasted_iota(jnp.int32, (128, length), 0).astype(f32) == slot
    request = 64.0 * matmul_nt(member[...], jnp.where(here, high, 0.0).astype(bf16))
    request += matmul_nt(member[...], jnp.where(here, low, 0.0).astype(bf16))
    ask[...] = request.astype(jnp.int32).reshape(ask.shape)

    pl.semaphore_wait(barrier, owners - 1)

    def send_ask(step, carry):
        other = lax.rem(me + step, owners)
        pltpu.make_async_remote_copy(
            src_ref=ask.at[other],
            dst_ref=asked_ref.at[me],
            send_sem=ask_send,
            recv_sem=ask_recv,
            device_id=device_of(other, emb_count),
            device_id_type=MESH,
        ).start()
        return carry

    lax.fori_loop(1, owners, send_ask, 0)
    z_copies = []
    for k in range(3):
        to = lax.rem(z_at + k + 1, 4)
        copy = pltpu.make_async_remote_copy(
            src_ref=weights_ref.at[:, z_at, core],
            dst_ref=weights_ref.at[:, z_at, core],
            send_sem=z_send.at[k],
            recv_sem=z_recv.at[k],
            device_id=(to * 2 + core, emb_at),
            device_id_type=MESH,
        )
        copy.start()
        z_copies.append(copy)
    asked_ref[me] = ask[me]

    table = key_heads.at[1]
    table_rows = table.shape[0]
    for number in range(4):
        table_loads[number].wait()

        def narrow(index, carry):
            at = pl.ds(pl.multiple_of(index * 256, 256), 256)
            to = pl.ds(pl.multiple_of(index * 256 + number * chunk, 256), 256)
            table[to, :] = wide[number][at, :].astype(bf16)
            return carry

        lax.fori_loop(0, chunk // 256, narrow, 0)
        if number == 0:
            table_loads[3].start()

    others = pl.ds(0, owners - 1)
    pltpu.make_async_copy(ask.at[others], ask.at[others], ask_send).wait()
    pltpu.make_async_copy(asked_ref.at[others], asked_ref.at[others], ask_recv).wait()

    group = 256 // capacity
    groups = owners // group

    def find(step, carry):
        index = lax.rem(me // group + step, groups)
        first_user = index * group
        wanted = asked_ref[pl.ds(first_user, group)].astype(f32)
        wanted = jnp.broadcast_to(wanted, (group, capacity, 128))
        same = lax.broadcasted_iota(jnp.int32, wanted.shape, 1) == lax.broadcasted_iota(
            jnp.int32, wanted.shape, 2
        )
        column = jnp.sum(jnp.where(same, wanted, 0.0), axis=2, keepdims=True)
        column = column.reshape(256, 1) - 1.0
        lane = lax.broadcasted_iota(jnp.int32, (256, 256), 1).astype(f32)
        total = jnp.zeros((256, table.shape[1]), f32)
        for first in range(0, table_rows, 256):
            pick = (lane + float(first) == column).astype(f32).astype(bf16)
            total += matmul(pick, table[first : first + 256, :])
        found[pl.ds(pl.multiple_of(index * 256, 256), 256), :] = total.astype(bf16)

        def send_rows(turn, carry):
            user = first_user + lax.rem(me + turn, group)

            @pl.when(user != me)
            def _():
                pltpu.make_async_remote_copy(
                    src_ref=found.at[pl.ds(user * capacity, capacity)],
                    dst_ref=returned_ref.at[pl.ds(me * capacity, capacity)],
                    send_sem=row_send,
                    recv_sem=row_recv,
                    device_id=device_of(user, emb_count),
                    device_id_type=MESH,
                ).start()

            return carry

        lax.fori_loop(0, group, send_rows, 0)
        return carry

    lax.fori_loop(0, groups, find, 0)
    own = pl.ds(pl.multiple_of(me * capacity, capacity), capacity)
    returned_ref[own, :] = found[own, :]

    for copy in z_copies:
        copy.wait()
    pair_copies = []
    for z in range(4):
        copy = pltpu.make_async_remote_copy(
            src_ref=weights_ref.at[:, z, core],
            dst_ref=weights_ref.at[:, z, core],
            send_sem=pair_send.at[z],
            recv_sem=pair_recv.at[z],
            device_id=(z_at * 2 + 1 - core, emb_at),
            device_id_type=MESH,
        )
        copy.start()
        pair_copies.append(copy)
    for copy in pair_copies:
        copy.wait()
    lines = pl.ds(0, (owners - 1) * capacity)
    pltpu.make_async_copy(found.at[lines], found.at[lines], row_send).wait()
    pltpu.make_async_copy(returned_ref.at[lines], returned_ref.at[lines], row_recv).wait()

    block = 256
    width = cotangent_ref.shape[1]
    blocks = length // block
    heads = width // DH
    slots = returned_ref.shape[0]
    layer_count = weights_ref.shape[0]
    head_of = lax.broadcasted_iota(jnp.int32, (heads, width), 1) // DH
    head_mask = (head_of == lax.broadcasted_iota(jnp.int32, (heads, width), 0)).astype(f32)
    head_mask = head_mask.astype(bf16)

    weights = weights_ref.reshape(layer_count, width, 5 * width)

    def rows(index):
        return pl.ds(pl.multiple_of(index * block, block), block)

    def head_rows(index):
        return pl.ds(pl.multiple_of(index * block * heads, block * heads), block * heads)

    def pair_of(query, key):
        return query * (query + 1) // 2 + key

    def fetch(index, carry):
        at = pl.multiple_of(index * 128, 128)
        column = to_column(target_ref[:, pl.ds(at, 128)].astype(f32))
        total = jnp.zeros((128, width), f32)
        for first in range(0, slots, 256):
            lane = lax.broadcasted_iota(jnp.int32, (128, 256), 1).astype(f32) + float(first)
            pick = (lane == column).astype(f32).astype(bf16)
            total += matmul(pick, returned_ref[first : first + 256, :])
        hidden[0, pl.ds(at, 128), :] = total.astype(bf16)
        return carry

    lax.fori_loop(0, length // 128, fetch, 0)

    def forward(layer, carry):
        def project(index, carry):
            at = rows(index)
            value = hidden[layer, at, :].astype(f32)
            center = value - jnp.mean(value, axis=1, keepdims=True)
            inverse = lax.rsqrt(jnp.mean(center * center, axis=1, keepdims=True) + EPSILON)
            norm = (center * inverse).astype(bf16)
            hidden_inv[layer, at, :] = inverse
            normed[layer, at, :] = norm
            for part in range(4):
                columns = slice(part * width, part * width + width)
                pre = matmul(norm, weights[layer, :, columns])
                logistic = 0.5 + 0.5 * jnp.tanh(0.5 * pre)
                act = pre * logistic
                slope[layer, at, columns] = (logistic + act - act * logistic).astype(bf16)
                act = act.astype(bf16)
                if part == 0:
                    gate[layer, at, :] = act
                elif part == 2:
                    queries[layer, at, :] = act * jnp.asarray(0.0625, bf16)
                else:
                    store = value_heads if part == 1 else key_heads
                    for head in range(heads):
                        spot = pl.ds(
                            pl.multiple_of((index * heads + head) * block, block), block
                        )
                        store[layer, spot, :] = act * head_mask[head : head + 1, :]
            return carry

        lax.fori_loop(0, blocks, project, 0)

        def scores(query, key, masked):
            pair = pair_of(query, key)
            query_part = queries[layer, rows(query), :]
            if masked:
                visible = lax.broadcasted_iota(
                    jnp.int32, (block, block), 1
                ) <= lax.broadcasted_iota(jnp.int32, (block, block), 0)
            parts = []
            for head in range(heads):
                spot = pl.ds(pl.multiple_of((key * heads + head) * block, block), block)
                half = matmul_nt(query_part, key_heads[layer, spot, :])
                bend = jnp.tanh(half)
                lift = 1.0 + bend
                if masked:
                    lift = jnp.where(visible, lift, 0.0)
                columns = slice(head * block, head * block + block)
                part = (half * lift).astype(bf16)
                parts.append(part)
                attn[layer, pair, :, columns] = part
                score_slope[layer, pair, :, columns] = (
                    lift * (1.0 + (half - half * bend))
                ).astype(bf16)
            return matmul(
                jnp.concatenate(parts, axis=1), value_heads[layer, head_rows(key), :]
            )

        def attend_rows(query, carry):
            mixture[...] = scores(query, query, True)

            def before(key, carry):
                mixture[...] += scores(query, key, False)
                return carry

            lax.fori_loop(0, query, before, 0)
            at = rows(query)
            value = mixture[...]
            center = value - jnp.mean(value, axis=1, keepdims=True)
            inverse = lax.rsqrt(jnp.mean(center * center, axis=1, keepdims=True) + EPSILON)
            norm = center * inverse
            mix_normed[layer, at, :] = norm
            mix_inv[layer, at, :] = inverse
            gated_part = (norm * gate[layer, at, :].astype(f32)).astype(bf16)
            gated[layer, at, :] = gated_part

            @pl.when(layer < layer_count - 1)
            def _():
                branch = matmul(gated_part, weights[layer, :, 4 * width :])
                hidden[layer + 1, at, :] = (hidden[layer, at, :].astype(f32) + branch).astype(bf16)

            return carry

        lax.fori_loop(0, blocks, attend_rows, 0)
        return carry

    lax.fori_loop(0, layer_count, forward, 0)

    cotangent_load.wait()
    gradient[...] = cotangent_ref[...].astype(f32)

    in_flight = {}

    def send(name, layer, number, source, place, where):
        copy = pltpu.make_async_remote_copy(
            src_ref=source,
            dst_ref=place,
            send_sem=reduce_send.at[layer, number],
            recv_sem=reduce_recv.at[layer, number],
            device_id=where,
            device_id_type=MESH,
        )
        copy.start()
        in_flight.setdefault((name, layer), []).append(copy)

    def receive(name, layer):
        for copy in in_flight[name, layer]:
            copy.wait()

    def reduce_pair(layer):
        where = (z_at * 2 + 1 - core, emb_at)
        send("pair", layer, 0, grads.at[layer, 1 - core], pair_in.at[layer], where)

    def reduce_z(layer):
        receive("pair", layer)
        for z in range(4):
            pair_in[layer, z] = (
                grads[layer, core, z].astype(f32) + pair_in[layer, z].astype(f32)
            ).astype(bf16)
        for k in range(3):
            to = lax.rem(z_at + k + 1, 4)
            where = (to * 2 + core, emb_at)
            send("z", layer, 1 + k, pair_in.at[layer, to], z_in.at[layer, k], where)

    def reduce_x(layer):
        receive("z", layer)
        half = z_sum.shape[3]
        for part in range(4):
            spot = slice(part // 2 * 16, part // 2 * 16 + 16)
            span = slice(part % 2 * half, part % 2 * half + half)
            value = pair_in[layer, z_at, spot, span].astype(f32)
            for k in range(3):
                value += z_in[layer, k, spot, span].astype(f32)
            z_sum[layer, part] = value.astype(bf16)
        for k in range(3):
            to = lax.rem(x_at + k + 1, 4)
            where = (fsdp_at, y_at * 4 + to)
            send("x", layer, 4 + k, z_sum.at[layer, to], x_in.at[layer, k], where)

    def reduce_y(layer):
        receive("x", layer)
        value = z_sum[layer, x_at].astype(f32)
        for k in range(3):
            value += x_in[layer, k].astype(f32)
        y_all[layer, y_at] = value.astype(bf16)
        for k in range(3):
            to = lax.rem(y_at + k + 1, 4)
            where = (fsdp_at, to * 4 + x_at)
            send("y", layer, 7 + k, y_all.at[layer, y_at], y_all.at[layer, y_at], where)

    def reduce_g(layer):
        receive("y", layer)
        value = y_all[layer, 0].astype(f32)
        for y in range(1, 4):
            value += y_all[layer, y].astype(f32)
        total_ref[layer, x_at] = value.astype(bf16)
        for k in range(3):
            to = lax.rem(x_at + k + 1, 4)
            where = (fsdp_at, y_at * 4 + to)
            place = total_ref.at[layer, x_at]
            send("g", layer, 10 + k, place, place, where)

    def reduce_end(layer):
        receive("g", layer)

    def backward(layer, between):

        def through_gate(index, carry):
            at = rows(index)
            grad_round = gradient[at, :].astype(bf16)
            grad_gated = matmul_nt(grad_round, weights[layer, :, 4 * width :])
            norm = mix_normed[layer, at, :]
            first = slope[layer, at, :width].astype(f32)
            grad_pre[at, :width] = (grad_gated * norm * first).astype(bf16)
            inner = grad_gated * gate[layer, at, :].astype(f32)
            grad = mix_inv[layer, at, :] * (
                inner
                - jnp.mean(inner, axis=1, keepdims=True)
                - norm * jnp.mean(inner * norm, axis=1, keepdims=True)
            )
            grad_mix[at, :] = grad.astype(bf16)
            grad_mix_t[:, at] = grad.T.astype(bf16)
            normed_t[:, at] = normed[layer, at, :].T
            queries_t[:, at] = queries[layer, at, :].T
            return carry

        lax.fori_loop(0, blocks, through_gate, 0)
        between[0]()

        gw_out = lax.dot_general(
            gated[layer],
            gradient[...].astype(bf16),
            (((0,), (0,)), ((), ())),
            preferred_element_type=jnp.float32,
        ).astype(bf16)
        depth = grads.shape[3]
        for part in range(8):
            grads[layer, part % 2, part // 2, :, 4 * width :] = gw_out[
                part * depth : part * depth + depth
            ]

        keys_t[...] = jnp.zeros_like(keys_t)
        values_t[...] = jnp.zeros_like(values_t)

        def through_scores(query, carry):
            mixture[...] = jnp.zeros_like(mixture)

            def one(key, carry):
                pair = pair_of(query, key)
                here = rows(query)
                there = rows(key)
                grad_part = grad_mix[here, :]
                parts = []
                for head in range(heads):
                    spot = pl.ds(pl.multiple_of((key * heads + head) * block, block), block)
                    columns = slice(head * block, head * block + block)
                    lines = slice(head * DH, head * DH + DH)
                    grad = matmul_nt(grad_part, value_heads[layer, spot, :])
                    values_t[lines, there] += matmul(
                        grad_mix_t[lines, here], attn[layer, pair, :, columns]
                    )
                    part = (grad * score_slope[layer, pair, :, columns].astype(f32)).astype(bf16)
                    parts.append(part)
                    keys_t[lines, there] += matmul(queries_t[lines, here], part)
                mixture[...] += matmul(
                    jnp.concatenate(parts, axis=1), key_heads[layer, head_rows(key), :]
                )
                return carry

            lax.fori_loop(0, query + 1, one, 0)
            at = rows(query)
            third = slope[layer, at, 2 * width : 3 * width].astype(f32)
            grad_pre[at, 2 * width : 3 * width] = (mixture[...] * 0.0625 * third).astype(bf16)
            return carry

        lax.fori_loop(0, blocks, through_scores, 0)
        between[1]()

        def through_keys(key, carry):
            at = rows(key)
            for part, total in ((1, values_t), (3, keys_t)):
                span = slice(part * width, part * width + width)
                grad_pre[at, span] = (total[:, at].T * slope[layer, at, span].astype(f32)).astype(
                    bf16
                )
            return carry

        lax.fori_loop(0, blocks, through_keys, 0)
        between[2]()

        for part in range(4):
            span = slice(part * width, part * width + width)
            gw_proj = matmul(normed_t[...], grad_pre[:, span]).astype(bf16)
            for piece in range(8):
                grads[layer, piece % 2, piece // 2, :, span] = gw_proj[
                    piece * depth : piece * depth + depth
                ]

        reduce_pair(layer)
        between[3]()

        def through_norm(index, carry):
            at = rows(index)
            grad_normed = matmul_nt(grad_pre[at, :], weights[layer, :, : 4 * width])
            norm = normed[layer, at, :].astype(f32)
            gradient[at, :] = gradient[at, :] + hidden_inv[layer, at, :] * (
                grad_normed
                - jnp.mean(grad_normed, axis=1, keepdims=True)
                - norm * jnp.mean(grad_normed * norm, axis=1, keepdims=True)
            )
            return carry

        lax.fori_loop(0, blocks, through_norm, 0)
    def nothing():
        pass

    backward(1, (nothing, nothing, nothing, nothing))
    backward(
        0,
        (
            lambda: reduce_z(1),
            lambda: reduce_x(1),
            lambda: reduce_y(1),
            lambda: reduce_g(1),
        ),
    )


    reduce_z(0)

    def give_back(step, carry):
        index = lax.rem(me * capacity // 128 + step, slots // 128)
        at = pl.ds(pl.multiple_of(index * 128, 128), 128)
        total = jnp.zeros((128, width), f32)
        for first in range(0, length, 256):
            spot = lax.broadcasted_iota(jnp.int32, (128, 256), 0) + index * 128
            pick = (spot == target_ref[:, first : first + 256]).astype(f32).astype(bf16)
            total += matmul(pick, gradient[first : first + 256, :].astype(bf16))
        found[at, :] = total.astype(bf16)
        return carry

    lax.fori_loop(0, slots // 128, give_back, 0)

    def send_grads(step, carry):
        other = lax.rem(me + step, owners)
        pltpu.make_async_remote_copy(
            src_ref=found.at[pl.ds(other * capacity, capacity)],
            dst_ref=incoming_ref.at[pl.ds(me * capacity, capacity)],
            send_sem=grad_send,
            recv_sem=grad_recv,
            device_id=device_of(other, emb_count),
            device_id_type=MESH,
        ).start()
        return carry

    lax.fori_loop(1, owners, send_grads, 0)
    incoming_ref[own, :] = found[own, :]
    reduce_x(0)
    reduce_end(1)
    reduce_y(0)
    reduce_g(0)
    reduce_end(0)
    pltpu.make_async_copy(found.at[lines], found.at[lines], grad_send).wait()
    pltpu.make_async_copy(incoming_ref.at[lines], incoming_ref.at[lines], grad_recv).wait()


def run_step(owner, offset, w_proj, w_out, table, cotangent, owners, emb_count, capacity):
    f32, bf16, i32 = jnp.float32, jnp.bfloat16, jnp.int32
    layer_count, depth, split = w_proj.shape
    columns = split + w_out.shape[2]
    length, width = cotangent.shape
    slots = owners * capacity
    blocks = length // 256
    pairs = blocks * (blocks + 1) // 2
    heads = width // DH
    two = layer_count
    vmem = pl.BlockSpec(memory_space=pltpu.VMEM)
    sem = pltpu.SemaphoreType.DMA
    scratch = [
        ((1, length), i32),
        ((1, length), i32),
        (w_proj.shape, bf16),
        (w_out.shape, bf16),
        ((length, width), bf16),
        ((slots, width), bf16),
        ((1, length), i32),
        ((two, 4, 2, depth, columns), bf16),
        ((owners, length), bf16),
        ((owners, 1, 128), i32),
        ((slots, width), bf16),
        ((two, length, width), bf16),
        ((two, length, 1), f32),
        ((two, length, width), bf16),
        ((two, length, split), bf16),
        ((two, length, width), bf16),
        ((two, length, width), bf16),
        ((two, length * heads, width), bf16),
        ((two, length * heads, width), bf16),
        ((two, pairs, 256, 256 * heads), bf16),
        ((two, pairs, 256, 256 * heads), bf16),
        ((two, length, width), f32),
        ((two, length, 1), f32),
        ((two, length, width), bf16),
        ((length, width), f32),
        ((256, width), f32),
        ((length, width), bf16),
        ((length, split), bf16),
        ((width, length), bf16),
        ((width, length), bf16),
        ((width, length), bf16),
        ((width, length), f32),
        ((width, length), f32),
        ((two, 2, 4, depth, columns), bf16),
        ((two, 4, depth, columns), bf16),
        ((two, 3, depth, columns), bf16),
        ((two, 4, 16, columns // 2), bf16),
        ((two, 3, 16, columns // 2), bf16),
        ((two, 4, 16, columns // 2), bf16),
    ]
    return pl.pallas_call(
        functools.partial(step_kernel, owners, emb_count, capacity),
        out_shape=(
            jax.ShapeDtypeStruct((slots, width), bf16),
            jax.ShapeDtypeStruct((owners, 1, 128), i32),
            jax.ShapeDtypeStruct((two, 4, 16, columns // 2), bf16),
        ),
        in_specs=[pl.BlockSpec(memory_space=pl.ANY)] * 6,
        out_specs=(vmem,) * 3,
        scratch_shapes=[pltpu.VMEM(*one) for one in scratch]
        + [sem((9,))]
        + [sem] * 6
        + [sem((3,)), sem((3,)), sem((4,)), sem((4,)), sem((two, 13)), sem((two, 13))],
        compiler_params=pltpu.CompilerParams(
            collective_id=1, has_side_effects=True, vmem_limit_bytes=62 << 20
        ),
        name="step",
    )(owner, offset, w_proj, w_out, table, cotangent)


def update_kernel(
    block, scale, table_ref, requested_ref, stale_ref, incoming_ref, total_ref, new_ref, proj_ref, out_ref
):
    @pl.when(pl.program_id(0) == 0)
    def _():
        half = total_ref.shape[3]
        split = proj_ref.shape[2]
        for part in range(4):
            spot = slice(part // 2 * 16, part // 2 * 16 + 16)
            value = total_ref[:, part].astype(jnp.float32) * scale
            if part % 2 == 0:
                proj_ref[:, spot, :half] = value
            else:
                proj_ref[:, spot, half:] = value[:, :, : split - half]
                out_ref[:, spot, :] = value[:, :, split - half :]

    count = requested_ref.shape[1]
    first = pl.program_id(0) * block
    row = first + lax.broadcasted_iota(jnp.int32, (block, count), 0)
    pick = (row == requested_ref[...]).astype(jnp.float32).astype(jnp.bfloat16)
    grad = jnp.dot(pick, incoming_ref[...], preferred_element_type=jnp.float32)
    rate = 0.5 / (1.0 + stale_ref[...].astype(jnp.float32))
    same = lax.broadcasted_iota(jnp.int32, (128, 128), 0) == lax.broadcasted_iota(
        jnp.int32, (128, 128), 1
    )
    for part in range(block // 128):
        rows = slice(part * 128, part * 128 + 128)
        spread = jnp.where(same, rate[0, part : part + 1, :], 0.0)
        column = jnp.sum(spread, axis=1, keepdims=True)
        new_ref[rows, :] = table_ref[rows, :] - column * grad[rows, :]


def update_table(table, requested, staleness, incoming, total, scale):
    rows, width = table.shape
    block = 512
    count = incoming.shape[0]
    parts = block // 128
    layer_count, _, depth, half = total.shape
    depth *= 2
    split = 2 * half - width
    whole = lambda *dims: pl.BlockSpec(dims, lambda i: (0,) * len(dims))
    return pl.pallas_call(
        functools.partial(update_kernel, block, scale),
        out_shape=(
            jax.ShapeDtypeStruct(table.shape, jnp.float32),
            jax.ShapeDtypeStruct((layer_count, depth, split), jnp.float32),
            jax.ShapeDtypeStruct((layer_count, depth, width), jnp.float32),
        ),
        grid=(rows // block,),
        in_specs=[
            pl.BlockSpec((block, width), lambda i: (i, 0)),
            whole(1, count),
            pl.BlockSpec((1, parts, 128), lambda i: (i, 0, 0)),
            whole(count, width),
            whole(*total.shape),
        ],
        out_specs=(
            pl.BlockSpec((block, width), lambda i: (i, 0)),
            whole(layer_count, depth, split),
            whole(layer_count, depth, width),
        ),
        compiler_params=pltpu.CompilerParams(vmem_limit_bytes=58 << 20),
        name="update_table",
    )(
        table,
        requested.reshape(1, count),
        staleness.reshape(rows // block, parts, 128),
        incoming,
        total,
    )


def local(item_table, item_owner, item_row, staleness, w_proj, w_out, out_grad):
    emb_count = lax.axis_size("emb")
    owners = lax.axis_size("fsdp") * emb_count
    length = item_row.shape[1]
    capacity = 2 * length // owners
    incoming, asked, total = run_step(
        item_owner.reshape(1, length),
        item_row,
        w_proj,
        w_out,
        item_table,
        out_grad[0],
        owners,
        emb_count,
        capacity,
    )
    requested = asked[:, 0, :capacity] - 1
    norm_scale = (owners * length) ** (-0.5)
    return update_table(item_table, requested, staleness, incoming, total, norm_scale)


def solution(mesh):
    return jax.shard_map(
        local,
        mesh=mesh,
        in_specs=(
            P(("fsdp", "emb"), None),
            P(("fsdp", "emb"), None, None),
            P(("fsdp", "emb"), None),
            P(("fsdp", "emb")),
            P(None, "fsdp", None),
            P(None, "fsdp", None),
            P(("fsdp", "emb"), None, None),
        ),
        out_specs=(P(("fsdp", "emb"), None), P(None, "fsdp", None), P(None, "fsdp", None)),
        check_vma=False,
    )
```

time: 224 us -> 133 us (0.59)
  local copies, waits for them, and re-layouts: 22.9 us -> 0.69 us
  blocking collectives: 17.8 us -> 0 us
  starting transfers between devices: 15.9 us -> 0 us
  between operations: 14.2 us -> 0.64 us
  waiting for transfers between devices: 9.37 us -> 0 us
  Pallas kernels: 138 us -> 130 us
  other arithmetic: 4.71 us -> 1.03 us
    all_gather x1 -> x0, blocking collectives: 17.8 us -> none  [local(): lax.all_gather(w_out, 'fsdp', axis=1, tiled=True)]
    all_to_all x2 -> x0, starting transfers between devices: 15.9 us -> none  [the longest x1 11.1 us: ask_owners(): lax.all_to_all(payload, ('fsdp', 'emb'), split_axis=0, concat_axis=0, til...]
    gather x1 -> x0, local copies, waits for them, and re-layouts: 8.83 us -> none  [local(): item_table[safe_rows]]
    all_to_all x2 -> x0, waiting for transfers between devices: 8.67 us -> none  [the longest x1 8.67 us: ask_owners(): lax.all_to_all(payload, ('fsdp', 'emb'), split_axis=0, concat_axis=0, til...]
    pallas_call x3 -> x2, Pallas kernels: 138 us -> 130 us  [the longest x1 121 us: run_step(): pl.pallas_call(functools.partial(step_kernel, owners, emb_count, capacity...]
    unnamed x14 -> x0, local copies, waits for them, and re-layouts: 5.73 us -> none
    scatter x1 -> x0, local copies, waits for them, and re-layouts: 4.48 us -> none  [local(): request = jnp.full((owners * capacity,), -1, jnp.int32).at[target].set(of...]
  transfers between devices with their start and end apart: 3 -> 0, of which waited for: 1 -> 0; matrix products, arithmetic and copies ran while one was open for 6% -> 0% of each run, Pallas kernels for 0% -> 0%
where the time goes in v2:
time: 133 us
  Pallas kernels  130 us (98%)
    pallas_call x1, Pallas kernels, run_step(): pl.pallas_call(functools.partial(step_kernel, owners, emb_count, capacity...  121 us
    pallas_call x1, Pallas kernels, update_table(): pl.pallas_call(functools.partial(update_kernel, block, scale), out_shape=...  9.73 us

profile of v2, /device:TPU:0, one launch (start us, length us, event | category | flops | bytes accessed | tf_op | source)
XLA Modules:
  0.0 132.8 jit_solution(348964702646711925)
XLA Ops:
  0.6 120.7 %step.1 = (bf16[2048,256]{1,0:T(8,128)(2,1)}, s32[128,1,128]{2,1,0:T(1,128)}, bf16[2,4,16,640]{3,2,1,0:T(8,128)(2,1)}) custom-call(s32[1,1024]{1,0:T(1,128)} %bitcast.5, s32[1,1024]{1,0:T(1,128)} %offset_hbm.1, bf16[2,32,1024]{2,1,0:T(8,128)(2,1)} %proj_hbm.1, bf16[2,32,256]{2,1,0:T(8,128)(2,1)} %out_hbm.1, f32[4096,256]{1,0:T(8,128)} %table_ref.1, ...), custom_call_target="tpu_custom_call" | custom-call | tf_op jit(solution)/shard_map/step/pallas_call | solution.py:712
  121.4 1.0 add_reduce_fusion
  122.4 0.7 sub.7.requested_ref
  123.1 9.7 %update_table.1 = (f32[4096,256]{1,0:T(8,128)}, f32[2,32,1024]{2,1,0:T(8,128)}, f32[2,32,256]{2,1,0:T(8,128)}) custom-call(f32[4096,256]{1,0:T(8,128)} %table_ref.1, s32[1,2048]{1,0:T(1,128)} %sub.7.requested_ref, s32[8,4,128]{2,1,0:T(4,128)} %bitcast.4, bf16[2048,256]{1,0:T(8,128)(2,1)} %get-tuple-element.7.incoming_ref, ...), custom_call_target="tpu_custom_call" | custom-call | tf_op jit(solution)/shard_map/update_table/pallas_call | solution.py:773

commit v3 on v2

--- a/solution.py
+++ b/solution.py
@@ -66,7 +66,7 @@
     table_hbm,
     cotangent_hbm,
     incoming_ref,
-    asked_ref,
+    requested_ref,
     total_ref,
     owner_ref,
     offset_ref,
@@ -78,6 +78,7 @@
     weights_ref,
     member,
     ask,
+    asked_ref,
     found,
     hidden,
     hidden_inv,
@@ -247,6 +248,12 @@
         )
         column = jnp.sum(jnp.where(same, wanted, 0.0), axis=2, keepdims=True)
         column = column.reshape(256, 1) - 1.0
+        diagonal = lax.broadcasted_iota(jnp.int32, (256, 256), 0) == lax.broadcasted_iota(
+            jnp.int32, (256, 256), 1
+        )
+        span = pl.ds(pl.multiple_of(index * 256, 256), 256)
+        line = jnp.sum(jnp.where(diagonal, column, 0.0), axis=0, keepdims=True)
+        requested_ref[:, span] = line.astype(jnp.int32)
         lane = lax.broadcasted_iota(jnp.int32, (256, 256), 1).astype(f32)
         total = jnp.zeros((256, table.shape[1]), f32)
         for first in range(0, table_rows, 256):
@@ -310,16 +317,20 @@
     weights = weights_ref.reshape(layer_count, width, 5 * width)
 
     def rows(index):
+        if isinstance(index, int):
+            return pl.ds(index * block, block)
         return pl.ds(pl.multiple_of(index * block, block), block)
 
     def head_rows(index):
+        if isinstance(index, int):
+            return pl.ds(index * block * heads, block * heads)
         return pl.ds(pl.multiple_of(index * block * heads, block * heads), block * heads)
 
     def pair_of(query, key):
         return query * (query + 1) // 2 + key
 
     def fetch(index, carry):
-        at = pl.multiple_of(index * 128, 128)
+        at = index * 128
         column = to_column(target_ref[:, pl.ds(at, 128)].astype(f32))
         total = jnp.zeros((128, width), f32)
         for first in range(0, slots, 256):
@@ -329,7 +340,8 @@
         hidden[0, pl.ds(at, 128), :] = total.astype(bf16)
         return carry
 
-    lax.fori_loop(0, length // 128, fetch, 0)
+    for at_index in range(length // 128):
+        fetch(at_index, 0)
 
     def forward(layer, carry):
         def project(index, carry):
@@ -354,36 +366,34 @@
                 else:
                     store = value_heads if part == 1 else key_heads
                     for head in range(heads):
-                        spot = pl.ds(
-                            pl.multiple_of((index * heads + head) * block, block), block
-                        )
+                        spot = rows(index * heads + head)
                         store[layer, spot, :] = act * head_mask[head : head + 1, :]
             return carry
 
-        lax.fori_loop(0, blocks, project, 0)
+        for at_index in range(0, blocks):
+            project(at_index, 0)
 
         def scores(query, key, masked):
             pair = pair_of(query, key)
             query_part = queries[layer, rows(query), :]
+            one = jnp.asarray(1.0, bf16)
             if masked:
                 visible = lax.broadcasted_iota(
                     jnp.int32, (block, block), 1
                 ) <= lax.broadcasted_iota(jnp.int32, (block, block), 0)
             parts = []
             for head in range(heads):
-                spot = pl.ds(pl.multiple_of((key * heads + head) * block, block), block)
-                half = matmul_nt(query_part, key_heads[layer, spot, :])
+                spot = rows(key * heads + head)
+                half = matmul_nt(query_part, key_heads[layer, spot, :]).astype(bf16)
                 bend = jnp.tanh(half)
-                lift = 1.0 + bend
+                lift = one + bend
                 if masked:
-                    lift = jnp.where(visible, lift, 0.0)
+                    lift = jnp.where(visible, lift, jnp.zeros_like(lift))
                 columns = slice(head * block, head * block + block)
-                part = (half * lift).astype(bf16)
+                part = half * lift
                 parts.append(part)
                 attn[layer, pair, :, columns] = part
-                score_slope[layer, pair, :, columns] = (
-                    lift * (1.0 + (half - half * bend))
-                ).astype(bf16)
+                score_slope[layer, pair, :, columns] = lift * (one + (half - half * bend))
             return matmul(
                 jnp.concatenate(parts, axis=1), value_heads[layer, head_rows(key), :]
             )
@@ -395,7 +405,8 @@
                 mixture[...] += scores(query, key, False)
                 return carry
 
-            lax.fori_loop(0, query, before, 0)
+            for at_index in range(0, query):
+                before(at_index, 0)
             at = rows(query)
             value = mixture[...]
             center = value - jnp.mean(value, axis=1, keepdims=True)
@@ -406,14 +417,13 @@
             gated_part = (norm * gate[layer, at, :].astype(f32)).astype(bf16)
             gated[layer, at, :] = gated_part
 
-            @pl.when(layer < layer_count - 1)
-            def _():
-                branch = matmul(gated_part, weights[layer, :, 4 * width :])
-                hidden[layer + 1, at, :] = (hidden[layer, at, :].astype(f32) + branch).astype(bf16)
-
+            branch = matmul(gated_part, weights[layer, :, 4 * width :])
+            following = lax.rem(layer + 1, layer_count)
+            hidden[following, at, :] = (hidden[layer, at, :].astype(f32) + branch).astype(bf16)
             return carry
 
-        lax.fori_loop(0, blocks, attend_rows, 0)
+        for at_index in range(0, blocks):
+            attend_rows(at_index, 0)
         return carry
 
     lax.fori_loop(0, layer_count, forward, 0)
@@ -516,7 +526,8 @@
             queries_t[:, at] = queries[layer, at, :].T
             return carry
 
-        lax.fori_loop(0, blocks, through_gate, 0)
+        for at_index in range(0, blocks):
+            through_gate(at_index, 0)
         between[0]()
 
         gw_out = lax.dot_general(
@@ -544,14 +555,14 @@
                 grad_part = grad_mix[here, :]
                 parts = []
                 for head in range(heads):
-                    spot = pl.ds(pl.multiple_of((key * heads + head) * block, block), block)
+                    spot = rows(key * heads + head)
                     columns = slice(head * block, head * block + block)
                     lines = slice(head * DH, head * DH + DH)
-                    grad = matmul_nt(grad_part, value_heads[layer, spot, :])
+                    grad = matmul_nt(grad_part, value_heads[layer, spot, :]).astype(bf16)
                     values_t[lines, there] += matmul(
                         grad_mix_t[lines, here], attn[layer, pair, :, columns]
                     )
-                    part = (grad * score_slope[layer, pair, :, columns].astype(f32)).astype(bf16)
+                    part = grad * score_slope[layer, pair, :, columns]
                     parts.append(part)
                     keys_t[lines, there] += matmul(queries_t[lines, here], part)
                 mixture[...] += matmul(
@@ -559,13 +570,15 @@
                 )
                 return carry
 
-            lax.fori_loop(0, query + 1, one, 0)
+            for at_index in range(0, query + 1):
+                one(at_index, 0)
             at = rows(query)
             third = slope[layer, at, 2 * width : 3 * width].astype(f32)
             grad_pre[at, 2 * width : 3 * width] = (mixture[...] * 0.0625 * third).astype(bf16)
             return carry
 
-        lax.fori_loop(0, blocks, through_scores, 0)
+        for at_index in range(0, blocks):
+            through_scores(at_index, 0)
         between[1]()
 
         def through_keys(key, carry):
@@ -577,7 +590,8 @@
                 )
             return carry
 
-        lax.fori_loop(0, blocks, through_keys, 0)
+        for at_index in range(0, blocks):
+            through_keys(at_index, 0)
         between[2]()
 
         for part in range(4):
@@ -602,7 +616,8 @@
             )
             return carry
 
-        lax.fori_loop(0, blocks, through_norm, 0)
+        for at_index in range(0, blocks):
+            through_norm(at_index, 0)
     def nothing():
         pass
 
@@ -620,18 +635,17 @@
 
     reduce_z(0)
 
-    def give_back(step, carry):
-        index = lax.rem(me * capacity // 128 + step, slots // 128)
-        at = pl.ds(pl.multiple_of(index * 128, 128), 128)
+    def give_back(index):
+        at = pl.ds(index * 128, 128)
         total = jnp.zeros((128, width), f32)
         for first in range(0, length, 256):
             spot = lax.broadcasted_iota(jnp.int32, (128, 256), 0) + index * 128
             pick = (spot == target_ref[:, first : first + 256]).astype(f32).astype(bf16)
             total += matmul(pick, gradient[first : first + 256, :].astype(bf16))
         found[at, :] = total.astype(bf16)
-        return carry
-
-    lax.fori_loop(0, slots // 128, give_back, 0)
+
+    for at_index in range(slots // 128):
+        give_back(at_index)
 
     def send_grads(step, carry):
         other = lax.rem(me + step, owners)
@@ -645,12 +659,15 @@
         ).start()
         return carry
 
-    lax.fori_loop(1, owners, send_grads, 0)
+    lax.fori_loop(1, 33, send_grads, 0)
+    reduce_x(0)
+    lax.fori_loop(33, 65, send_grads, 0)
+    reduce_y(0)
+    lax.fori_loop(65, 97, send_grads, 0)
+    reduce_g(0)
+    lax.fori_loop(97, owners, send_grads, 0)
     incoming_ref[own, :] = found[own, :]
-    reduce_x(0)
     reduce_end(1)
-    reduce_y(0)
-    reduce_g(0)
     reduce_end(0)
     pltpu.make_async_copy(found.at[lines], found.at[lines], grad_send).wait()
     pltpu.make_async_copy(incoming_ref.at[lines], incoming_ref.at[lines], grad_recv).wait()
@@ -678,6 +695,7 @@
         ((1, length), i32),
         ((two, 4, 2, depth, columns), bf16),
         ((owners, length), bf16),
+        ((owners, 1, 128), i32),
         ((owners, 1, 128), i32),
         ((slots, width), bf16),
         ((two, length, width), bf16),
@@ -713,7 +731,7 @@
         functools.partial(step_kernel, owners, emb_count, capacity),
         out_shape=(
             jax.ShapeDtypeStruct((slots, width), bf16),
-            jax.ShapeDtypeStruct((owners, 1, 128), i32),
+            jax.ShapeDtypeStruct((1, slots), i32),
             jax.ShapeDtypeStruct((two, 4, 16, columns // 2), bf16),
         ),
         in_specs=[pl.BlockSpec(memory_space=pl.ANY)] * 6,
@@ -794,7 +812,7 @@
         name="update_table",
     )(
         table,
-        requested.reshape(1, count),
+        requested,
         staleness.reshape(rows // block, parts, 128),
         incoming,
         total,
@@ -806,7 +824,7 @@
     owners = lax.axis_size("fsdp") * emb_count
     length = item_row.shape[1]
     capacity = 2 * length // owners
-    incoming, asked, total = run_step(
+    incoming, requested, total = run_step(
         item_owner.reshape(1, length),
         item_row,
         w_proj,
@@ -817,7 +835,6 @@
         emb_count,
         capacity,
     )
-    requested = asked[:, 0, :capacity] - 1
     norm_scale = (owners * length) ** (-0.5)
     return update_table(item_table, requested, staleness, incoming, total, norm_scale)
 

time: 133 us -> 116 us (0.87)
  Pallas kernels: 130 us -> 115 us
    pallas_call x1, Pallas kernels: 121 us -> 105 us  [run_step(): pl.pallas_call(functools.partial(step_kernel, owners, emb_count, capacity...]
where the time goes in v3:
time: 116 us
  Pallas kernels  115 us (99%)
    pallas_call x1, Pallas kernels, run_step(): pl.pallas_call(functools.partial(step_kernel, owners, emb_count, capacity...  105 us
    pallas_call x1, Pallas kernels, update_table(): pl.pallas_call(functools.partial(update_kernel, block, scale), out_shape=...  9.75 us

profile of v3, /device:TPU:0, one launch (start us, length us, event | category | flops | bytes accessed | tf_op | source)
XLA Modules:
  0.0 115.6 jit_solution(6678215956140232819)
XLA Ops:
  0.6 105.2 %step.1 = (bf16[2048,256]{1,0:T(8,128)(2,1)}, s32[1,2048]{1,0:T(1,128)}, bf16[2,4,16,640]{3,2,1,0:T(8,128)(2,1)}) custom-call(s32[1,1024]{1,0:T(1,128)} %bitcast.5, s32[1,1024]{1,0:T(1,128)} %offset_hbm.1, bf16[2,32,1024]{2,1,0:T(8,128)(2,1)} %proj_hbm.1, bf16[2,32,256]{2,1,0:T(8,128)(2,1)} %out_hbm.1, f32[4096,256]{1,0:T(8,128)} %table_ref.1, ...), custom_call_target="tpu_custom_call" | custom-call | tf_op jit(solution)/shard_map/step/pallas_call | solution.py:730
  105.9 9.8 %update_table.1 = (f32[4096,256]{1,0:T(8,128)}, f32[2,32,1024]{2,1,0:T(8,128)}, f32[2,32,256]{2,1,0:T(8,128)}) custom-call(f32[4096,256]{1,0:T(8,128)} %table_ref.1, s32[1,2048]{1,0:T(1,128)} %get-tuple-element.6.requested_ref, s32[8,4,128]{2,1,0:T(4,128)} %bitcast.4, bf16[2048,256]{1,0:T(8,128)(2,1)} %get-tuple-element.7.incoming_ref, ...), custom_call_target="tpu_custom_call" | custom-call | tf_op jit(solution)/shard_map/update_table/pallas_call | solution.py:791

commit v4 on v3

--- a/solution.py
+++ b/solution.py
@@ -281,6 +281,16 @@
         return carry
 
     lax.fori_loop(0, groups, find, 0)
+    picks = attn.at[0]
+    across = picks.shape[2]
+    all_slots = owners * capacity
+    for part in range(length // 128):
+        place = to_column(target_ref[:, part * 128 : part * 128 + 128].astype(f32))
+        for first in range(0, all_slots, 256):
+            lane = lax.broadcasted_iota(jnp.int32, (128, 256), 1).astype(f32) + float(first)
+            line = first // across * 128
+            span = slice(first % across, first % across + 256)
+            picks[part, line : line + 128, span] = (lane == place).astype(f32).astype(bf16)
     own = pl.ds(pl.multiple_of(me * capacity, capacity), capacity)
     returned_ref[own, :] = found[own, :]
 
@@ -329,19 +339,15 @@
     def pair_of(query, key):
         return query * (query + 1) // 2 + key
 
-    def fetch(index, carry):
-        at = index * 128
-        column = to_column(target_ref[:, pl.ds(at, 128)].astype(f32))
+    def fetch(part, carry):
         total = jnp.zeros((128, width), f32)
-        for first in range(0, slots, 256):
-            lane = lax.broadcasted_iota(jnp.int32, (128, 256), 1).astype(f32) + float(first)
-            pick = (lane == column).astype(f32).astype(bf16)
-            total += matmul(pick, returned_ref[first : first + 256, :])
-        hidden[0, pl.ds(at, 128), :] = total.astype(bf16)
+        for first in range(0, slots, across):
+            line = first // across * 128
+            total += matmul(picks[part, line : line + 128, :], returned_ref[first : first + across, :])
+        hidden[0, pl.ds(pl.multiple_of(part * 128, 128), 128), :] = total.astype(bf16)
         return carry
 
-    for at_index in range(length // 128):
-        fetch(at_index, 0)
+    lax.fori_loop(0, length // 128, fetch, 0)
 
     def forward(layer, carry):
         def project(index, carry):
@@ -464,46 +470,47 @@
             where = (to * 2 + core, emb_at)
             send("z", layer, 1 + k, pair_in.at[layer, to], z_in.at[layer, k], where)
 
-    def reduce_x(layer):
-        receive("z", layer)
+    def reduce_x():
+        for layer in range(layer_count):
+            receive("z", layer)
         half = z_sum.shape[3]
-        for part in range(4):
-            spot = slice(part // 2 * 16, part // 2 * 16 + 16)
-            span = slice(part % 2 * half, part % 2 * half + half)
-            value = pair_in[layer, z_at, spot, span].astype(f32)
-            for k in range(3):
-                value += z_in[layer, k, spot, span].astype(f32)
-            z_sum[layer, part] = value.astype(bf16)
+        for layer in range(layer_count):
+            for part in range(4):
+                spot = slice(part // 2 * 16, part // 2 * 16 + 16)
+                span = slice(part % 2 * half, part % 2 * half + half)
+                value = pair_in[layer, z_at, spot, span].astype(f32)
+                for k in range(3):
+                    value += z_in[layer, k, spot, span].astype(f32)
+                z_sum[layer, part] = value.astype(bf16)
         for k in range(3):
             to = lax.rem(x_at + k + 1, 4)
             where = (fsdp_at, y_at * 4 + to)
-            send("x", layer, 4 + k, z_sum.at[layer, to], x_in.at[layer, k], where)
-
-    def reduce_y(layer):
-        receive("x", layer)
-        value = z_sum[layer, x_at].astype(f32)
-        for k in range(3):
-            value += x_in[layer, k].astype(f32)
-        y_all[layer, y_at] = value.astype(bf16)
+            send("x", 0, 4 + k, z_sum.at[:, to], x_in.at[:, k], where)
+
+    def reduce_y():
+        receive("x", 0)
+        for layer in range(layer_count):
+            value = z_sum[layer, x_at].astype(f32)
+            for k in range(3):
+                value += x_in[layer, k].astype(f32)
+            y_all[layer, y_at] = value.astype(bf16)
         for k in range(3):
             to = lax.rem(y_at + k + 1, 4)
             where = (fsdp_at, to * 4 + x_at)
-            send("y", layer, 7 + k, y_all.at[layer, y_at], y_all.at[layer, y_at], where)
-
-    def reduce_g(layer):
-        receive("y", layer)
-        value = y_all[layer, 0].astype(f32)
-        for y in range(1, 4):
-            value += y_all[layer, y].astype(f32)
-        total_ref[layer, x_at] = value.astype(bf16)
+            send("y", 0, 7 + k, y_all.at[:, y_at], y_all.at[:, y_at], where)
+
+    def reduce_g():
+        receive("y", 0)
+        for layer in range(layer_count):
+            value = y_all[layer, 0].astype(f32)
+            for y in range(1, 4):
+                value += y_all[layer, y].astype(f32)
+            total_ref[layer, x_at] = value.astype(bf16)
         for k in range(3):
             to = lax.rem(x_at + k + 1, 4)
             where = (fsdp_at, y_at * 4 + to)
-            place = total_ref.at[layer, x_at]
-            send("g", layer, 10 + k, place, place, where)
-
-    def reduce_end(layer):
-        receive("g", layer)
+            place = total_ref.at[:, x_at]
+            send("g", 0, 10 + k, place, place, where)
 
     def backward(layer, between):
 
@@ -622,15 +629,7 @@
         pass
 
     backward(1, (nothing, nothing, nothing, nothing))
-    backward(
-        0,
-        (
-            lambda: reduce_z(1),
-            lambda: reduce_x(1),
-            lambda: reduce_y(1),
-            lambda: reduce_g(1),
-        ),
-    )
+    backward(0, (lambda: reduce_z(1), nothing, nothing, nothing))
 
 
     reduce_z(0)
@@ -659,16 +658,15 @@
         ).start()
         return carry
 
-    lax.fori_loop(1, 33, send_grads, 0)
-    reduce_x(0)
-    lax.fori_loop(33, 65, send_grads, 0)
-    reduce_y(0)
-    lax.fori_loop(65, 97, send_grads, 0)
-    reduce_g(0)
-    lax.fori_loop(97, owners, send_grads, 0)
+    lax.fori_loop(1, 17, send_grads, 0)
+    reduce_x()
+    lax.fori_loop(17, 49, send_grads, 0)
+    reduce_y()
+    lax.fori_loop(49, 89, send_grads, 0)
+    reduce_g()
+    lax.fori_loop(89, owners, send_grads, 0)
     incoming_ref[own, :] = found[own, :]
-    reduce_end(1)
-    reduce_end(0)
+    receive("g", 0)
     pltpu.make_async_copy(found.at[lines], found.at[lines], grad_send).wait()
     pltpu.make_async_copy(incoming_ref.at[lines], incoming_ref.at[lines], grad_recv).wait()
 
@@ -781,7 +779,7 @@
 
 def update_table(table, requested, staleness, incoming, total, scale):
     rows, width = table.shape
-    block = 512
+    block = 1024
     count = incoming.shape[0]
     parts = block // 128
     layer_count, _, depth, half = total.shape

time: 116 us -> 109 us (0.940)
  Pallas kernels: 115 us -> 108 us
    pallas_call x1, Pallas kernels: 105 us -> 100 us  [run_step(): pl.pallas_call(functools.partial(step_kernel, owners, emb_count, capacity...]
    pallas_call x1, Pallas kernels: 9.75 us -> 8.09 us  [update_table(): pl.pallas_call(functools.partial(update_kernel, block, scale), out_shape=...]
where the time goes in v4:
time: 109 us
  Pallas kernels  108 us (99%)
    pallas_call x1, Pallas kernels, run_step(): pl.pallas_call(functools.partial(step_kernel, owners, emb_count, capacity...  100 us
    pallas_call x1, Pallas kernels, update_table(): pl.pallas_call(functools.partial(update_kernel, block, scale), out_shape=...  8.09 us

profile of v4, /device:TPU:0, one launch (start us, length us, event | category | flops | bytes accessed | tf_op | source)
XLA Modules:
  0.0 108.8 jit_solution(10143389348803231697)
XLA Ops:
  0.6 100.1 %step.1 = (bf16[2048,256]{1,0:T(8,128)(2,1)}, s32[1,2048]{1,0:T(1,128)}, bf16[2,4,16,640]{3,2,1,0:T(8,128)(2,1)}) custom-call(s32[1,1024]{1,0:T(1,128)} %bitcast.5, s32[1,1024]{1,0:T(1,128)} %offset_hbm.1, bf16[2,32,1024]{2,1,0:T(8,128)(2,1)} %proj_hbm.1, bf16[2,32,256]{2,1,0:T(8,128)(2,1)} %out_hbm.1, f32[4096,256]{1,0:T(8,128)} %table_ref.1, ...), custom_call_target="tpu_custom_call" | custom-call | tf_op jit(solution)/shard_map/step/pallas_call | solution.py:728
  100.7 8.1 %update_table.1 = (f32[4096,256]{1,0:T(8,128)}, f32[2,32,1024]{2,1,0:T(8,128)}, f32[2,32,256]{2,1,0:T(8,128)}) custom-call(f32[4096,256]{1,0:T(8,128)} %table_ref.1, s32[1,2048]{1,0:T(1,128)} %get-tuple-element.6.requested_ref, s32[4,8,128]{2,1,0:T(8,128)} %bitcast.4, bf16[2048,256]{1,0:T(8,128)(2,1)} %get-tuple-element.7.incoming_ref, ...), custom_call_target="tpu_custom_call" | custom-call | tf_op jit(solution)/shard_map/update_table/pallas_call | solution.py:789

commit v5 on v4

--- a/solution.py
+++ b/solution.py
@@ -284,13 +284,15 @@
     picks = attn.at[0]
     across = picks.shape[2]
     all_slots = owners * capacity
-    for part in range(length // 128):
-        place = to_column(target_ref[:, part * 128 : part * 128 + 128].astype(f32))
+    halves = all_slots // across
+    for part in range(length // 256):
+        place = to_column(target_ref[:, part * 256 : part * 256 + 256].astype(f32))
         for first in range(0, all_slots, 256):
-            lane = lax.broadcasted_iota(jnp.int32, (128, 256), 1).astype(f32) + float(first)
-            line = first // across * 128
+            lane = lax.broadcasted_iota(jnp.int32, (256, 256), 1).astype(f32) + float(first)
             span = slice(first % across, first % across + 256)
-            picks[part, line : line + 128, span] = (lane == place).astype(f32).astype(bf16)
+            picks[part * halves + first // across, :, span] = (
+                (lane == place).astype(f32).astype(bf16)
+            )
     own = pl.ds(pl.multiple_of(me * capacity, capacity), capacity)
     returned_ref[own, :] = found[own, :]
 
@@ -340,14 +342,15 @@
         return query * (query + 1) // 2 + key
 
     def fetch(part, carry):
-        total = jnp.zeros((128, width), f32)
-        for first in range(0, slots, across):
-            line = first // across * 128
-            total += matmul(picks[part, line : line + 128, :], returned_ref[first : first + across, :])
-        hidden[0, pl.ds(pl.multiple_of(part * 128, 128), 128), :] = total.astype(bf16)
+        total = jnp.zeros((256, width), f32)
+        for half in range(halves):
+            total += matmul(
+                picks[part * halves + half], returned_ref[half * across : half * across + across, :]
+            )
+        hidden[0, rows(part), :] = total.astype(bf16)
         return carry
 
-    lax.fori_loop(0, length // 128, fetch, 0)
+    lax.fori_loop(0, length // 256, fetch, 0)
 
     def forward(layer, carry):
         def project(index, carry):
@@ -362,9 +365,9 @@
                 columns = slice(part * width, part * width + width)
                 pre = matmul(norm, weights[layer, :, columns])
                 logistic = 0.5 + 0.5 * jnp.tanh(0.5 * pre)
-                act = pre * logistic
-                slope[layer, at, columns] = (logistic + act - act * logistic).astype(bf16)
-                act = act.astype(bf16)
+                act = (pre * logistic).astype(bf16)
+                logistic = logistic.astype(bf16)
+                slope[layer, at, columns] = logistic + (act - act * logistic)
                 if part == 0:
                     gate[layer, at, :] = act
                 elif part == 2:
@@ -635,15 +638,17 @@
     reduce_z(0)
 
     def give_back(index):
-        at = pl.ds(index * 128, 128)
-        total = jnp.zeros((128, width), f32)
-        for first in range(0, length, 256):
-            spot = lax.broadcasted_iota(jnp.int32, (128, 256), 0) + index * 128
-            pick = (spot == target_ref[:, first : first + 256]).astype(f32).astype(bf16)
-            total += matmul(pick, gradient[first : first + 256, :].astype(bf16))
-        found[at, :] = total.astype(bf16)
-
-    for at_index in range(slots // 128):
+        at = pl.ds(index * 256, 256)
+        spot = lax.broadcasted_iota(jnp.int32, (256, 256), 0) + index * 256
+        parts = [
+            (spot == target_ref[:, first : first + 256]).astype(f32).astype(bf16)
+            for first in range(0, length, 256)
+        ]
+        found[at, :] = matmul(
+            jnp.concatenate(parts, axis=1), gradient[...].astype(bf16)
+        ).astype(bf16)
+
+    for at_index in range(slots // 256):
         give_back(at_index)
 
     def send_grads(step, carry):

time: 109 us -> 108 us (level)
  no operation moved by 1% of the time
where the time goes in v5:
time: 108 us
  Pallas kernels  107 us (99%)
    pallas_call x1, Pallas kernels, run_step(): pl.pallas_call(functools.partial(step_kernel, owners, emb_count, capacity...  99.4 us
    pallas_call x1, Pallas kernels, update_table(): pl.pallas_call(functools.partial(update_kernel, block, scale), out_shape=...  8.09 us

profile of v5, /device:TPU:0, one launch (start us, length us, event | category | flops | bytes accessed | tf_op | source)
XLA Modules:
  0.0 108.1 jit_solution(4459825649817746584)
XLA Ops:
  0.6 99.4 %step.1 = (bf16[2048,256]{1,0:T(8,128)(2,1)}, s32[1,2048]{1,0:T(1,128)}, bf16[2,4,16,640]{3,2,1,0:T(8,128)(2,1)}) custom-call(s32[1,1024]{1,0:T(1,128)} %bitcast.5, s32[1,1024]{1,0:T(1,128)} %offset_hbm.1, bf16[2,32,1024]{2,1,0:T(8,128)(2,1)} %proj_hbm.1, bf16[2,32,256]{2,1,0:T(8,128)(2,1)} %out_hbm.1, f32[4096,256]{1,0:T(8,128)} %table_ref.1, ...), custom_call_target="tpu_custom_call" | custom-call | tf_op jit(solution)/shard_map/step/pallas_call | solution.py:733
  100.0 8.1 %update_table.1 = (f32[4096,256]{1,0:T(8,128)}, f32[2,32,1024]{2,1,0:T(8,128)}, f32[2,32,256]{2,1,0:T(8,128)}) custom-call(f32[4096,256]{1,0:T(8,128)} %table_ref.1, s32[1,2048]{1,0:T(1,128)} %get-tuple-element.6.requested_ref, s32[4,8,128]{2,1,0:T(8,128)} %bitcast.4, bf16[2048,256]{1,0:T(8,128)(2,1)} %get-tuple-element.7.incoming_ref, ...), custom_call_target="tpu_custom_call" | custom-call | tf_op jit(solution)/shard_map/update_table/pallas_call | solution.py:794

commit v6 on v5

--- a/solution.py
+++ b/solution.py
@@ -604,15 +604,18 @@
             through_keys(at_index, 0)
         between[2]()
 
-        for part in range(4):
-            span = slice(part * width, part * width + width)
-            gw_proj = matmul(normed_t[...], grad_pre[:, span]).astype(bf16)
-            for piece in range(8):
-                grads[layer, piece % 2, piece // 2, :, span] = gw_proj[
-                    piece * depth : piece * depth + depth
-                ]
-
-        reduce_pair(layer)
+        def weigh():
+            for part in range(4):
+                span = slice(part * width, part * width + width)
+                gw_proj = matmul(normed_t[...], grad_pre[:, span]).astype(bf16)
+                for piece in range(8):
+                    grads[layer, piece % 2, piece // 2, :, span] = gw_proj[
+                        piece * depth : piece * depth + depth
+                    ]
+            reduce_pair(layer)
+
+        if layer > 0:
+            weigh()
         between[3]()
 
         def through_norm(index, carry):
@@ -628,14 +631,13 @@
 
         for at_index in range(0, blocks):
             through_norm(at_index, 0)
+        return weigh
     def nothing():
         pass
 
     backward(1, (nothing, nothing, nothing, nothing))
-    backward(0, (lambda: reduce_z(1), nothing, nothing, nothing))
-
-
-    reduce_z(0)
+    weigh_first = backward(0, (lambda: reduce_z(1), nothing, nothing, nothing))
+
 
     def give_back(index):
         at = pl.ds(index * 256, 256)
@@ -663,9 +665,11 @@
         ).start()
         return carry
 
-    lax.fori_loop(1, 17, send_grads, 0)
+    lax.fori_loop(1, 33, send_grads, 0)
+    weigh_first()
+    reduce_z(0)
     reduce_x()
-    lax.fori_loop(17, 49, send_grads, 0)
+    lax.fori_loop(33, 49, send_grads, 0)
     reduce_y()
     lax.fori_loop(49, 89, send_grads, 0)
     reduce_g()

time: 108 us -> 111 us (1.028)
  Pallas kernels: 107 us -> 110 us
    pallas_call x1, Pallas kernels: 99.4 us -> 102 us  [run_step(): pl.pallas_call(functools.partial(step_kernel, owners, emb_count, capacity...]
where the time goes in v6:
time: 111 us
  Pallas kernels  110 us (99%)
    pallas_call x1, Pallas kernels, run_step(): pl.pallas_call(functools.partial(step_kernel, owners, emb_count, capacity...  102 us
    pallas_call x1, Pallas kernels, update_table(): pl.pallas_call(functools.partial(update_kernel, block, scale), out_shape=...  8.09 us

profile of v6, /device:TPU:0, one launch (start us, length us, event | category | flops | bytes accessed | tf_op | source)
XLA Modules:
  0.0 110.6 jit_solution(8402698703918964010)
XLA Ops:
  0.6 101.9 %step.1 = (bf16[2048,256]{1,0:T(8,128)(2,1)}, s32[1,2048]{1,0:T(1,128)}, bf16[2,4,16,640]{3,2,1,0:T(8,128)(2,1)}) custom-call(s32[1,1024]{1,0:T(1,128)} %bitcast.5, s32[1,1024]{1,0:T(1,128)} %offset_hbm.1, bf16[2,32,1024]{2,1,0:T(8,128)(2,1)} %proj_hbm.1, bf16[2,32,256]{2,1,0:T(8,128)(2,1)} %out_hbm.1, f32[4096,256]{1,0:T(8,128)} %table_ref.1, ...), custom_call_target="tpu_custom_call" | custom-call | tf_op jit(solution)/shard_map/step/pallas_call | solution.py:737
  102.6 8.1 %update_table.1 = (f32[4096,256]{1,0:T(8,128)}, f32[2,32,1024]{2,1,0:T(8,128)}, f32[2,32,256]{2,1,0:T(8,128)}) custom-call(f32[4096,256]{1,0:T(8,128)} %table_ref.1, s32[1,2048]{1,0:T(1,128)} %get-tuple-element.6.requested_ref, s32[4,8,128]{2,1,0:T(8,128)} %bitcast.4, bf16[2048,256]{1,0:T(8,128)(2,1)} %get-tuple-element.7.incoming_ref, ...), custom_call_target="tpu_custom_call" | custom-call | tf_op jit(solution)/shard_map/update_table/pallas_call | solution.py:798
